TPU v7x, 256 devices: a whole 4x4x8 slice. The times are simulated.
256 devices in a mesh: grp: 8 (over y, core), dev: 32 (over x, z).
Axes of the slice: x: 4, y: 4, z: 8, core: 2. Of those that a mesh axis runs over, the one named last changes fastest.
Arguments:
- particle_pos: float32 [2, 4194304], P(None, ('grp', 'dev')), may hold values from -1 to 1
- particle_mass: float32 [4194304], P(('grp', 'dev')), may hold values from 0.02 to 0.2
- leaf_counts: int32 [65536], P(('grp', 'dev')), may hold values from 1 to 64, 3145728 in all
Outputs:
- lens_field: float32 [4, 4194304], P(None, ('grp', 'dev'))
Inputs may be any that keep to these rules, and one draw needn't show every extreme that they name: `leaf_counts`: every leaf holds 1 to 64 live particles and some leaf exactly 64; the counts sum to 3145728.
All inputs are finite; a program needn't handle non-finite values. No bound on the sum of `leaf_counts` on one device may be relied on, other than what follows from the above.
Results may differ from a plain program's by a relative error of at most 0.0001.
Values sent between devices are 32-bit elements; how exact they have to be, the bound alone decides.
A program may use at most 192 MiB of HBM per device.

v0:
```python
import jax
import jax.numpy as jnp
from jax import lax
from jax.sharding import PartitionSpec as P

NODES = 6
PPL = 64
LSIDE = 16


SOFTEN = 0.01
PRECISE = lax.Precision.HIGHEST


def partner(block, axis, distance):
    count = lax.axis_size(axis)
    route = []
    for low in range(count):
        high = low | 1 << distance
        if high != low and high < count:
            route += [(low, high), (high, low)]
    return lax.ppermute(block, axis, route)


def node_angles():
    return (2.0 * jnp.arange(NODES, dtype=jnp.float32) + 1.0) * (jnp.pi / (2.0 * NODES))


def cheb_points():
    return jnp.cos(node_angles())


def interp_basis(coords):
    angles = node_angles()
    expand = (slice(None),) + (None,) * coords.ndim
    result = jnp.zeros((NODES,) + coords.shape, jnp.float32) + 1.0 / NODES
    lower_poly = jnp.ones_like(coords)
    upper_poly = coords
    for degree in range(1, NODES):
        at_nodes = jnp.cos(degree * angles)
        result = result + 2.0 / NODES * at_nodes[expand] * upper_poly[None]
        lower_poly, upper_poly = (upper_poly, 2.0 * coords * upper_poly - lower_poly)
    return result


def kernel_vals(delta_x, delta_y):
    inv_r2 = 1.0 / (delta_x * delta_x + delta_y * delta_y + SOFTEN)
    inv_sq = inv_r2 * inv_r2
    return (
        delta_x * inv_r2,
        delta_y * inv_r2,
        (delta_y * delta_y - delta_x * delta_x) * inv_sq,
        -2.0 * delta_x * delta_y * inv_sq,
    )


def far_offsets():
    return [
        (off_x, off_y)
        for off_x in range(-3, 4)
        for off_y in range(-3, 4)
        if max(abs(off_x), abs(off_y)) >= 2
    ]


def transfer_table(half_width, off_x, off_y):
    points = cheb_points()
    node_diff = points[:, None] - points[None, :]
    delta_x = half_width * node_diff[:, None, :, None] - 2.0 * half_width * off_x
    delta_y = half_width * node_diff[None, :, None, :] - 2.0 * half_width * off_y
    kernel_set = kernel_vals(delta_x, delta_y)
    stacked = jnp.stack([term_val for term_val in kernel_set])
    return stacked.reshape(4 * NODES * NODES, NODES * NODES)


def pair_mask(size_x, size_y, off_x, off_y):
    cells_x = jnp.arange(size_x, dtype=jnp.int32)
    cells_y = jnp.arange(size_y, dtype=jnp.int32)
    keep_x = jnp.abs((cells_x + off_x) // 2 - cells_x // 2) <= 1
    keep_y = jnp.abs((cells_y + off_y) // 2 - cells_y // 2) <= 1
    return (keep_x[:, None] & keep_y[None, :]).astype(jnp.float32)


def far_field(padded, size_x, size_y, half_width):
    result = jnp.zeros((4 * NODES * NODES, size_x * size_y), jnp.float32)
    for off_x, off_y in far_offsets():
        shifted = (
            padded[:, 3 + off_x : 3 + off_x + size_x, 3 + off_y : 3 + off_y + size_y]
            * pair_mask(size_x, size_y, off_x, off_y)[None]
        )
        result = result + jnp.dot(
            transfer_table(half_width, off_x, off_y),
            shifted.reshape(NODES * NODES, size_x * size_y),
            precision=PRECISE,
            preferred_element_type=jnp.float32,
        )
    return result.reshape(4, NODES * NODES, size_x, size_y)


def child_table():
    points = cheb_points()
    sides = jnp.arange(2, dtype=jnp.float32)
    coords = -0.5 + sides[:, None] + 0.5 * points[None, :]
    per_side = jnp.transpose(interp_basis(coords), (1, 2, 0))
    product_table = per_side[:, None, :, None, :, None] * per_side[None, :, None, :, None, :]
    return product_table.reshape(2, 2, NODES * NODES, NODES * NODES)


def upward(leaf_grid):
    node_table = child_table()
    size_x = leaf_grid.shape[1] // 2
    size_y = leaf_grid.shape[2] // 2
    result = jnp.zeros((NODES * NODES, size_x * size_y), jnp.float32)
    for side_x in (0, 1):
        for side_y in (0, 1):
            child_part = leaf_grid[:, side_x::2, side_y::2].reshape(NODES * NODES, size_x * size_y)
            result = result + jnp.dot(
                node_table[side_x, side_y].T,
                child_part,
                precision=PRECISE,
                preferred_element_type=jnp.float32,
            )
    return result.reshape(NODES * NODES, size_x, size_y)


def downward(parent_local):
    node_table = child_table()
    size_x = parent_local.shape[2]
    size_y = parent_local.shape[3]
    flat_local = jnp.transpose(parent_local, (1, 0, 2, 3)).reshape(
        NODES * NODES, 4 * size_x * size_y
    )
    row_list = []
    for side_x in (0, 1):
        col_list = []
        for side_y in (0, 1):
            child_part = jnp.dot(
                node_table[side_x, side_y],
                flat_local,
                precision=PRECISE,
                preferred_element_type=jnp.float32,
            )
            col_list.append(child_part.reshape(NODES * NODES, 4, size_x, size_y))
        row_list.append(jnp.stack(col_list, axis=-1))
    stacked = jnp.stack(row_list, axis=3).reshape(NODES * NODES, 4, 2 * size_x, 2 * size_y)
    return jnp.transpose(stacked, (1, 0, 2, 3))


def moments(grid_u, grid_v, grid_w):
    basis_u = interp_basis(grid_u) * grid_w[None]
    basis_v = interp_basis(grid_v)
    result = jnp.einsum("axyp,bxyp->abxy", basis_u, basis_v, precision=PRECISE)
    return result.reshape(NODES * NODES, grid_u.shape[0], grid_u.shape[1])


def near_row(target_u, target_v, near_rows):
    size_y = target_u.shape[0]
    blocks = []
    shift_x = []
    shift_y = []
    for off_x in (-1, 0, 1):
        for off_y in (-1, 0, 1):
            blocks.append(near_rows[:, off_x + 1, off_y + 1 : off_y + 1 + size_y, :])
            shift_x.append(jnp.full((PPL,), -off_x, jnp.float32))
            shift_y.append(jnp.full((PPL,), -off_y, jnp.float32))
    sources = jnp.concatenate(blocks, axis=2)
    delta_x = jnp.concatenate(shift_x)[None, None, :] + 0.5 * (
        target_u[:, :, None] - sources[0][:, None, :]
    )
    delta_y = jnp.concatenate(shift_y)[None, None, :] + 0.5 * (
        target_v[:, :, None] - sources[1][:, None, :]
    )
    weight = sources[2][:, None, :]
    return jnp.stack(
        [jnp.sum(weight * term_val, axis=2) for term_val in kernel_vals(delta_x, delta_y)]
    )


def evaluate_row(target_u, target_v, local_row, near_rows):
    basis_u = interp_basis(target_u)
    basis_v = interp_basis(target_v)
    coeffs = local_row.reshape(4, NODES, NODES, target_u.shape[0])
    half_sum = jnp.einsum("cabq,bqp->caqp", coeffs, basis_v, precision=PRECISE)
    far_part = jnp.sum(half_sum * basis_u[None], axis=1)
    return far_part + near_row(target_u, target_v, near_rows)


def leaves_to_grid(values, axis_pos, bit_count):
    x_bits = (bit_count + 1) // 2
    y_bits = bit_count // 2
    old_shape = values.shape
    split_vals = values.reshape(old_shape[:axis_pos] + (2,) * bit_count + old_shape[axis_pos + 1 :])
    x_dims = [axis_pos + bit_count - 1 - 2 * bit_level for bit_level in range(x_bits - 1, -1, -1)]
    y_dims = [axis_pos + bit_count - 2 - 2 * bit_level for bit_level in range(y_bits - 1, -1, -1)]
    lead_dims = list(range(axis_pos))
    tail_dims = list(range(axis_pos + bit_count, split_vals.ndim))
    permuted = jnp.transpose(split_vals, lead_dims + x_dims + y_dims + tail_dims)
    return permuted.reshape(
        old_shape[:axis_pos] + (2**x_bits, 2**y_bits) + old_shape[axis_pos + 1 :]
    )


def grid_to_leaves(values, axis_pos, bit_count):
    x_bits = (bit_count + 1) // 2
    y_bits = bit_count // 2
    old_shape = values.shape
    split_vals = values.reshape(old_shape[:axis_pos] + (2,) * bit_count + old_shape[axis_pos + 2 :])
    order_dims = []
    for bit_level in range(bit_count - 1, -1, -1):
        if bit_level % 2 == 0:
            order_dims.append(axis_pos + x_bits - 1 - bit_level // 2)
        else:
            order_dims.append(axis_pos + x_bits + y_bits - 1 - (bit_level - 1) // 2)
    lead_dims = list(range(axis_pos))
    tail_dims = list(range(axis_pos + bit_count, split_vals.ndim))
    permuted = jnp.transpose(split_vals, lead_dims + order_dims + tail_dims)
    return permuted.reshape(old_shape[:axis_pos] + (2**bit_count,) + old_shape[axis_pos + 2 :])


def morton_split(code_val, bit_count):
    coord_x = code_val * 0
    coord_y = code_val * 0
    for bit_level in range((bit_count + 1) // 2):
        coord_x = coord_x + code_val // 4**bit_level % 2 * 2**bit_level
        coord_y = coord_y + code_val // (2 * 4**bit_level) % 2 * 2**bit_level
    return (coord_x, coord_y)


def cut_moments(moment_grid, strip_kind):
    if strip_kind == 0:
        return moment_grid[:, :3, :]
    if strip_kind == 1:
        return moment_grid[:, -3:, :]
    if strip_kind == 2:
        return jnp.swapaxes(moment_grid[:, :, :3], 1, 2)
    return jnp.swapaxes(moment_grid[:, :, -3:], 1, 2)


def cut_particles(particles, strip_kind):
    if strip_kind == 0:
        return particles[:, 0]
    if strip_kind == 1:
        return particles[:, -1]
    if strip_kind == 2:
        return particles[:, :, 0]
    return particles[:, :, -1]


def corner(strip_vals, off_x, off_y, use_x):
    along_y = strip_vals[:, :, -3:] if off_y < 0 else strip_vals[:, :, :3]
    along_x = strip_vals[:, :, -3:] if off_x < 0 else strip_vals[:, :, :3]
    return jnp.where(use_x, along_y, jnp.swapaxes(along_x, 1, 2))


def dot_corner(strip_vals, off_x, off_y, use_x):
    from_x = strip_vals[:, -1] if off_y < 0 else strip_vals[:, 0]
    from_y = strip_vals[:, -1] if off_x < 0 else strip_vals[:, 0]
    return jnp.where(use_x, from_x, from_y)[:, None, None]


def swap_bit(values, code_bit, dev_bits):
    if code_bit < dev_bits:
        return partner(values, "dev", code_bit)
    return partner(values, "grp", code_bit - dev_bits)


def on_device(particle_pos, particle_mass, leaf_counts):
    grp_count = lax.axis_size("grp")
    dev_count = lax.axis_size("dev")
    block_bits = (grp_count * dev_count).bit_length() - 1
    dev_bits = dev_count.bit_length() - 1
    local_bits = 2 * (LSIDE.bit_length() - 1)
    side_par = LSIDE // 2
    blocks_x = 2 ** ((block_bits + 1) // 2)
    blocks_y = 2 ** (block_bits // 2)
    live_mask = (jnp.arange(PPL, dtype=jnp.int32)[None, :] < leaf_counts[:, None]).astype(
        jnp.float32
    )
    mass_rows = particle_mass.reshape(LSIDE * LSIDE, PPL)
    mass_sum, live_sum = lax.psum(
        (jnp.sum(mass_rows * live_mask), jnp.sum(live_mask)), ("grp", "dev")
    )
    mean_mass = mass_sum / live_sum
    weights = (mass_rows - mean_mass) * live_mask
    positions = particle_pos.reshape(2, LSIDE * LSIDE, PPL)
    grid_u = leaves_to_grid(positions[0], 0, local_bits)
    grid_v = leaves_to_grid(positions[1], 0, local_bits)
    grid_w = leaves_to_grid(weights, 0, local_bits)
    leaf_moments = moments(grid_u, grid_v, grid_w)
    parent_moments = upward(leaf_moments)
    particles = jnp.stack([grid_u, grid_v, grid_w])
    packed = jnp.stack(
        [
            jnp.concatenate(
                [
                    cut_moments(leaf_moments, strip_kind).ravel(),
                    cut_moments(parent_moments, strip_kind).ravel(),
                    cut_particles(particles, strip_kind).ravel(),
                ]
            )
            for strip_kind in range(4)
        ]
    )
    leaf_len = NODES * NODES * 3 * LSIDE
    par_len = NODES * NODES * 3 * side_par

    def unpack(vector):
        return (
            vector[:leaf_len].reshape(NODES * NODES, 3, LSIDE),
            vector[leaf_len : leaf_len + par_len].reshape(NODES * NODES, 3, side_par),
            vector[leaf_len + par_len :].reshape(3, LSIDE, PPL),
        )

    block_id = lax.axis_index("grp") * dev_count + lax.axis_index("dev")
    block_x, block_y = morton_split(block_id, block_bits)
    x_carry = jnp.stack([packed[1], packed[0]])
    for bit_level in range((block_bits + 1) // 2):
        taken = swap_bit(x_carry, 2 * bit_level, dev_bits)
        low_part = block_x % 2**bit_level
        x_carry = jnp.stack(
            [
                jnp.where(low_part == 0, taken[0], x_carry[0]),
                jnp.where(low_part == 2**bit_level - 1, taken[1], x_carry[1]),
            ]
        )
    y_carry = jnp.stack(
        [
            jnp.stack([packed[3], x_carry[0], x_carry[1]]),
            jnp.stack([packed[2], x_carry[0], x_carry[1]]),
        ]
    )
    for bit_level in range(block_bits // 2):
        taken = swap_bit(y_carry, 2 * bit_level + 1, dev_bits)
        low_part = block_y % 2**bit_level
        y_carry = jnp.stack(
            [
                jnp.where(low_part == 0, taken[0], y_carry[0]),
                jnp.where(low_part == 2**bit_level - 1, taken[1], y_carry[1]),
            ]
        )
    near_vecs = {
        (-1, 0): x_carry[0],
        (1, 0): x_carry[1],
        (0, -1): y_carry[0, 0],
        (0, 1): y_carry[1, 0],
        (-1, -1): y_carry[0, 1],
        (1, -1): y_carry[0, 2],
        (-1, 1): y_carry[1, 1],
        (1, 1): y_carry[1, 2],
    }

    def edge_vector(off_x, off_y):
        return near_vecs[off_x, off_y]

    tile_map = {(0, 0): (leaf_moments, parent_moments, particles)}
    for off_x in (-1, 0, 1):
        for off_y in (-1, 0, 1):
            if off_x == 0 and off_y == 0:
                continue
            near_x = block_x + off_x
            near_y = block_y + off_y
            inside = (
                (near_x >= 0) & (near_x < blocks_x) & (near_y >= 0) & (near_y < blocks_y)
            ).astype(jnp.float32)
            if off_y == 0:
                leaf_part, par_part, dot_part = unpack(edge_vector(off_x, off_y))
                pieces = (leaf_part, par_part, dot_part[:, None])
            elif off_x == 0:
                leaf_part, par_part, dot_part = unpack(edge_vector(off_x, off_y))
                pieces = (
                    jnp.swapaxes(leaf_part, 1, 2),
                    jnp.swapaxes(par_part, 1, 2),
                    dot_part[:, :, None],
                )
            else:
                vector = near_vecs[off_x, off_y]
                use_x = True
                leaf_part, par_part, dot_part = unpack(vector)
                pieces = (
                    corner(leaf_part, off_x, off_y, use_x),
                    corner(par_part, off_x, off_y, use_x),
                    dot_corner(dot_part, off_x, off_y, use_x),
                )
            tile_map[off_x, off_y] = tuple((piece_val * inside for piece_val in pieces))
    windows = []
    for member in range(3):
        columns = [
            jnp.concatenate([tile_map[off_x, off_y][member] for off_y in (-1, 0, 1)], axis=2)
            for off_x in (-1, 0, 1)
        ]
        windows.append(jnp.concatenate(columns, axis=1))
    leaf_window, par_window, part_window = windows
    parent_local = far_field(par_window, side_par, side_par, 1.0)
    leaf_local = far_field(leaf_window, LSIDE, LSIDE, 0.5) + downward(parent_local)

    def one_row(row_idx):
        near_rows = lax.dynamic_slice_in_dim(part_window, row_idx, 3, 1)
        target_u = lax.dynamic_index_in_dim(grid_u, row_idx, 0, keepdims=False)
        target_v = lax.dynamic_index_in_dim(grid_v, row_idx, 0, keepdims=False)
        local_row = lax.dynamic_index_in_dim(leaf_local, row_idx, 2, keepdims=False)
        return evaluate_row(target_u, target_v, local_row, near_rows)

    fields = lax.map(one_row, jnp.arange(LSIDE, dtype=jnp.int32))
    fields = jnp.transpose(fields, (1, 0, 2, 3))
    return grid_to_leaves(fields, 1, local_bits).reshape(4, LSIDE * LSIDE * PPL)


def solution(mesh):
    in_specs = (P(None, ("grp", "dev")), P(("grp", "dev")), P(("grp", "dev")))
    out_specs = P(None, ("grp", "dev"))
    return jax.shard_map(
        on_device, mesh=mesh, in_specs=in_specs, out_specs=out_specs, check_vma=False
    )
```

profile of v0, /device:TPU:1, one launch (start us, length us, event | category | flops | bytes accessed | tf_op | source)
XLA Modules:
  0.0 526.9 jit_solution(16787211099503064006)
XLA Ops:
  5.6 81.5 %all-reduce = (f32[]{:T(128)}, f32[]{:T(128)}) all-reduce(f32[]{:T(128)} %select_reduce_fusion, f32[]{:T(128)} %convert_reduce_fusion), channel_id=1, replica_groups=mesh['grp'=8,'dev'=32] {'grp','dev'}, use_global_device_ids=true, to_apply=%region_1.0 | all-reduce | flops 2 | bytes 16 | tf_op jit(solution)/shard_map/psum | solution.py:280
  88.8 2.6 convolution_bitcast_fusion.1
  98.2 12.1 %collective-permute-start = (f32[2,5664]{1,0:T(2,128)}, f32[2,5664]{1,0:T(2,128)}, u32[]{:S(2)}, u32[]{:S(2)}) collective-permute-start(f32[2,5664]{1,0:T(2,128)} %pad_maximum_fusion.90), channel_id=1, source_target_pairs={{0,1},{1,0},{2,3},{3,2},{4,5},{5,4},{6,7},{7,6},{8,9},{9,8},{10,11... | collective-permute-start | bytes 135944 | tf_op jit(solution)/shard_map/ppermute | solution.py:22
  112.8 2.4 broadcast_multiply_fusion.70
  115.2 3.5 broadcast_multiply_fusion.71
  119.5 3.1 broadcast_multiply_fusion.150
  122.7 4.1 broadcast_multiply_fusion.151
  175.8 3.3 collective-permute-start.1
  179.7 3.3 collective-permute-done.1
  186.9 3.0 collective-permute-done.2
  216.3 2.6 pad_maximum_fusion.2
  218.8 3.4 collective-permute-done.4
  223.5 3.1 collective-permute-done.5
  228.1 6.2 %collective-permute-start.6 = (f32[2,3,5664]{2,1,0:T(4,128)}, f32[2,3,5664]{2,1,0:T(4,128)}, u32[]{:S(2)}, u32[]{:S(2)}) collective-permute-start(f32[2,3,5664]{2,1,0:T(4,128)} %pad_maximum_fusion.82), channel_id=1, source_target_pairs={{0,32},{32,0},{64,96},{96,64},{128,160},{160,128},{192,224},{224,1... | collective-permute-start | bytes 407816 | tf_op jit(solution)/shard_map/ppermute | solution.py:22
  237.0 1.9 reshape.8441
  239.0 1.9 reshape.8435
  240.9 1.9 reshape.8431
  244.7 1.9 reshape.8421
  246.6 1.9 reshape.8417
  248.5 1.9 reshape.8411
  252.4 1.9 reshape.8403
  254.3 1.9 reshape.8391
  256.2 1.9 reshape.8387
  258.1 1.9 reshape.8381
  260.1 1.9 reshape.8377
  262.0 1.9 reshape.8373
  265.9 1.9 reshape.8369
  267.8 1.9 reshape.8371
  269.7 1.9 reshape.8375
  271.6 1.9 reshape.8379
  273.5 1.9 reshape.8383
  275.4 1.9 reshape.8385
  277.4 1.9 reshape.8389
  279.3 1.9 reshape.8393
  281.2 1.9 reshape.8395
  283.1 1.9 reshape.8397
  285.0 1.9 reshape.8399
  286.9 1.9 reshape.8401
  288.9 1.9 reshape.8405
  290.8 1.9 reshape.8409
  292.7 1.9 reshape.8415
  294.6 1.9 reshape.8419
  296.6 1.9 reshape.8423
  298.5 1.9 reshape.8425
  323.1 2.0 reshape.8284
  335.0 2.1 collective-permute-start.7
  338.2 4.8 collective-permute-done.7
  381.5 143.4 %while.13 = (s32[]{:T(128)}, f32[16,4,16,64]{3,1,2,0:T(4,128)S(1)}, s32[16]{0:T(128)S(1)}, f32[16,16,64]{2,1,0:T(8,128)S(1)}, f32[4,36,16,16]{1,0,3,2:T(4,128)S(...) while((s32[]{:T(128)}, f32[16,4,16,64]{3,1,2,0:T(4,128)S(1)}, ...), condition=%wide.region_10.11_spmd, body=%wide.region_4.10_spmd.sunk | while | flops 17893484 | bytes 1122444 | solution.py:403
  387.1 3.6 multiply_reduce_fusion.5
  396.0 3.6 multiply_reduce_fusion.5
  405.0 3.6 multiply_reduce_fusion.5
  413.9 3.6 multiply_reduce_fusion.5
  422.8 3.6 multiply_reduce_fusion.5
  431.8 3.6 multiply_reduce_fusion.5
  440.7 3.6 multiply_reduce_fusion.5
  449.7 3.6 multiply_reduce_fusion.5
  458.6 3.6 multiply_reduce_fusion.5
  467.6 3.6 multiply_reduce_fusion.5
  476.5 3.6 multiply_reduce_fusion.5
  485.4 3.6 multiply_reduce_fusion.5
  494.4 3.6 multiply_reduce_fusion.5
  503.3 3.6 multiply_reduce_fusion.5
  512.3 3.6 multiply_reduce_fusion.5
  521.2 3.6 multiply_reduce_fusion.5
  (1115 shorter events, 209.6 us)
Async XLA Ops:
  88.8 8.1 %copy-start.40 = (f32[2,2,2,2,2,2,2,2,64]{8,7,6,5,4,3,2,1,0:T(2,128)}, f32[2,2,2,2,2,2,2,2,64]{8,7,6,5,4,3,2,1,0:T(2,128)S(1)}, u32[]{:S(2)}) copy-start(f32[2,2,2,2,2,2,2,2,64]{8,7,6,5,4,3,2,1,0:T(2,128)S(1)} %copy.346) | copy-start | bytes 196612
  95.5 16.4 %copy-start.47 = (f32[2,2,36,36]{3,2,1,0:T(8,128)}, f32[2,2,36,36]{3,2,1,0:T(8,128)S(1)}, u32[]{:S(2)}) copy-start(f32[2,2,36,36]{3,2,1,0:T(8,128)S(1)} %broadcast_multiply_fusion.153) | copy-start | bytes 62212
  98.2 77.6 %collective-permute-start = (f32[2,5664]{1,0:T(2,128)}, f32[2,5664]{1,0:T(2,128)}, u32[]{:S(2)}, u32[]{:S(2)}) collective-permute-start(f32[2,5664]{1,0:T(2,128)} %pad_maximum_fusion.90), channel_id=1, source_target_pairs={{0,1},{1,0},{2,3},{3,2},{4,5},{5,4},{6,7},{7,6},{8,9},{9,8},{10,11... | collective-permute-start | bytes 135944 | tf_op jit(solution)/shard_map/ppermute | solution.py:22
  175.8 7.1 %collective-permute-start.1 = (f32[2,5664]{1,0:T(2,128)}, f32[2,5664]{1,0:T(2,128)}, u32[]{:S(2)}, u32[]{:S(2)}) collective-permute-start(f32[2,5664]{1,0:T(2,128)} %collective-permute-done), channel_id=1, source_target_pairs={{0,4},{4,0},{1,5},{5,1},{2,6},{6,2},{3,7},{7,3},{8,12},{12,8},{9,1... | collective-permute-start | bytes 135944 | tf_op jit(solution)/shard_map/ppermute | solution.py:22
  185.2 4.7 collective-permute-start.2
  192.1 21.0 %collective-permute-start.3 = (f32[2,5664]{1,0:T(2,128)}, f32[2,5664]{1,0:T(2,128)}, u32[]{:S(2)}, u32[]{:S(2)}) collective-permute-start(f32[2,5664]{1,0:T(2,128)} %pad_maximum_fusion.92), channel_id=1, source_target_pairs={{0,64},{64,0},{32,96},{96,32},{128,192},{192,128},{160,224},{224,1... | collective-permute-start | bytes 135944 | tf_op jit(solution)/shard_map/ppermute | solution.py:22
  214.9 7.3 %collective-permute-start.4 = (f32[2,3,5664]{2,1,0:T(4,128)S(1)}, f32[2,3,5664]{2,1,0:T(4,128)S(1)}, u32[]{:S(2)}, u32[]{:S(2)}) collective-permute-start(f32[2,3,5664]{2,1,0:T(4,128)S(1)} %pad_maximum_fusion.81), channel_id=1, source_target_pairs={{0,2},{2,0},{1,3},{3,1},{4,6},{6,4},{5,7},{7,5},{8,10},{10,8},{9,1... | collective-permute-start | bytes 407816 | tf_op jit(solution)/shard_map/ppermute | solution.py:22
  216.2 6.1 %copy-start.49 = (f32[1,6,6,6,6]{2,1,0,4,3:T(8,128)S(1)}, f32[1,6,6,6,6]{2,1,0,4,3:T(8,128)}, u32[]{:S(2)}) copy-start(f32[1,6,6,6,6]{2,1,0,4,3:T(8,128)} %get-tuple-element.528) | copy-start | bytes 15556
  216.2 6.1 %copy-start.50 = (f32[1,6,6,6,6]{2,1,0,4,3:T(8,128)S(1)}, f32[1,6,6,6,6]{2,1,0,4,3:T(8,128)}, u32[]{:S(2)}) copy-start(f32[1,6,6,6,6]{2,1,0,4,3:T(8,128)} %get-tuple-element.542) | copy-start | bytes 15556
  216.2 6.1 %copy-start.51 = (f32[1,6,6,6,6]{2,1,0,4,3:T(8,128)S(1)}, f32[1,6,6,6,6]{2,1,0,4,3:T(8,128)}, u32[]{:S(2)}) copy-start(f32[1,6,6,6,6]{2,1,0,4,3:T(8,128)} %get-tuple-element.543) | copy-start | bytes 15556
  216.2 6.1 %copy-start.52 = (f32[1,6,6,6,6]{2,1,0,4,3:T(8,128)S(1)}, f32[1,6,6,6,6]{2,1,0,4,3:T(8,128)}, u32[]{:S(2)}) copy-start(f32[1,6,6,6,6]{2,1,0,4,3:T(8,128)} %get-tuple-element.546) | copy-start | bytes 15556
  216.2 6.1 %copy-start.53 = (f32[1,6,6,6,6]{2,1,0,4,3:T(8,128)S(1)}, f32[1,6,6,6,6]{2,1,0,4,3:T(8,128)}, u32[]{:S(2)}) copy-start(f32[1,6,6,6,6]{2,1,0,4,3:T(8,128)} %get-tuple-element.673) | copy-start | bytes 15556
  216.2 6.1 %copy-start.54 = (f32[1,6,6,6,6]{2,1,0,4,3:T(8,128)S(1)}, f32[1,6,6,6,6]{2,1,0,4,3:T(8,128)}, u32[]{:S(2)}) copy-start(f32[1,6,6,6,6]{2,1,0,4,3:T(8,128)} %get-tuple-element.827) | copy-start | bytes 15556
  216.2 6.1 %copy-start.55 = (f32[1,6,6,6,6]{2,1,0,4,3:T(8,128)S(1)}, f32[1,6,6,6,6]{2,1,0,4,3:T(8,128)}, u32[]{:S(2)}) copy-start(f32[1,6,6,6,6]{2,1,0,4,3:T(8,128)} %get-tuple-element.828) | copy-start | bytes 15556
  216.2 6.1 %copy-start.56 = (f32[1,6,6,6,6]{2,1,0,4,3:T(8,128)S(1)}, f32[1,6,6,6,6]{2,1,0,4,3:T(8,128)}, u32[]{:S(2)}) copy-start(f32[1,6,6,6,6]{2,1,0,4,3:T(8,128)} %get-tuple-element.836) | copy-start | bytes 15556
  222.3 4.4 collective-permute-start.5
  228.1 105.8 %collective-permute-start.6 = (f32[2,3,5664]{2,1,0:T(4,128)}, f32[2,3,5664]{2,1,0:T(4,128)}, u32[]{:S(2)}, u32[]{:S(2)}) collective-permute-start(f32[2,3,5664]{2,1,0:T(4,128)} %pad_maximum_fusion.82), channel_id=1, source_target_pairs={{0,32},{32,0},{64,96},{96,64},{128,160},{160,128},{192,224},{224,1... | collective-permute-start | bytes 407816 | tf_op jit(solution)/shard_map/ppermute | solution.py:22
  321.4 3.7 copy-start.35
  322.3 3.7 copy-start.32
  323.1 3.7 copy-start.30
  335.0 8.0 %collective-permute-start.7 = (f32[2,3,5664]{2,1,0:T(4,128)S(1)}, f32[2,3,5664]{2,1,0:T(4,128)S(1)}, u32[]{:S(2)}, u32[]{:S(2)}) collective-permute-start(f32[2,3,5664]{2,1,0:T(4,128)S(1)} %pad_maximum_fusion.83), channel_id=1, source_target_pairs={{0,128},{128,0},{32,160},{160,32},{64,192},{192,64},{96,224},{224,... | collective-permute-start | bytes 407816 | tf_op jit(solution)/shard_map/ppermute | solution.py:22
  345.1 3.0 copy-start.184
  345.1 3.0 copy-start.256
  345.4 3.0 copy-start.175
  345.4 3.0 copy-start.243
  345.7 3.0 copy-start.163
  345.8 3.0 copy-start.242
  346.0 3.0 copy-start.173
  346.1 3.0 copy-start.241
  346.4 3.0 copy-start.172
  346.4 3.0 copy-start.240
  346.7 3.0 copy-start.171
  346.7 3.0 copy-start.239
  347.0 3.0 copy-start.170
  347.0 3.0 copy-start.238
  347.3 3.0 copy-start.169
  347.3 3.0 copy-start.237
  347.6 3.0 copy-start.156
  347.9 3.0 copy-start.167
  348.2 3.0 copy-start.153
  348.2 3.0 copy-start.255
  348.5 3.0 copy-start.166
  348.8 3.0 copy-start.152
  348.8 3.0 copy-start.236
  349.1 3.0 copy-start.165
  349.1 3.0 copy-start.235
  349.4 3.0 copy-start.151
  349.4 3.0 copy-start.234
  349.7 3.0 copy-start.164
  349.7 3.0 copy-start.233
  350.0 3.0 copy-start.150
  350.0 3.0 copy-start.232
  350.3 3.0 copy-start.162
  350.3 3.0 copy-start.231
  350.6 3.0 copy-start.161
  350.6 3.0 copy-start.230
  350.9 3.0 copy-start.183
  351.2 3.0 copy-start.160
  351.2 3.0 copy-start.229
  351.5 3.0 copy-start.149
  351.5 3.0 copy-start.228
  351.8 3.0 copy-start.159
  351.8 3.0 copy-start.227
  352.1 3.0 copy-start.148
  (205 other events, 353.6 us)
where the time goes:
time: 537 us; the launch traced here: 527 us
  local copies, waits for them, and re-layouts  160 us (30%)
  other arithmetic  145 us (27%)
  blocking collectives  81.5 us (15%)
  loops' own time  53.4 us (10%)
  matrix products  37.4 us (7%)
  starting transfers between devices  26.2 us (5%)
  waiting for transfers between devices  17.6 us (3%)
  between operations  5.99 us (1%)
    reshape x80, local copies, waits for them, and re-layouts, transfer_table(): return stacked.reshape(4 * NODES * NODES, NODES * NODES)  97.1 us
    psum x1, blocking collectives, on_device(): lax.psum((jnp.sum(mass_rows * live_mask), jnp.sum(live_mask)), ('grp', 'd...  81.5 us
    reduce_sum x16, other arithmetic, near_row(): jnp.sum(weight * term_val, axis=2)  57.3 us
    another operation x1, loops' own time, on_device(): fields = lax.map(one_row, jnp.arange(LSIDE, dtype=jnp.int32))  53.4 us
    another operation x40, other arithmetic, transfer_table(): stacked = jnp.stack([term_val for term_val in kernel_set])  48.1 us
    ppermute x8, starting transfers between devices, partner(): return lax.ppermute(block, axis, route)  26.2 us
    dot_general x80, matrix products, far_field(): jnp.dot(transfer_table(half_width, off_x, off_y), shifted.reshape(NODES *...  24.8 us
    ppermute x8, waiting for transfers between devices, partner(): return lax.ppermute(block, axis, route)  17.6 us
  transfers between devices with their start and end apart: 8, of which 5 were waited for; matrix products, arithmetic and copies ran while one was open for 36% of the time, Pallas kernels for 0%

commit v1 on v0

v1 whole, which is shorter than its diff:
```python
import functools

import jax
import jax.numpy as jnp
import numpy as np
from jax import lax
from jax.experimental import pallas as pl
from jax.experimental.pallas import tpu as pltpu
from jax.sharding import PartitionSpec as P

NODES = 6
PPL = 64
LSIDE = 16
SOFTEN = 0.01
NM = 40
HIGHEST = lax.Precision.HIGHEST
F32 = jnp.float32
BF16 = jnp.bfloat16

DIRS = ((-1, 0), (1, 0), (0, -1), (0, 1), (-1, -1), (1, -1), (-1, 1), (1, 1))
ROW_OF = (0, 16, 32, 48, 64, 72, 80, 88)
ROWS_IN = (16, 16, 16, 16, 8, 8, 8, 8)
HROWS = 128
LANES_OUT = 512
OFFS = tuple((ox, oy) for ox in (-1, 0, 1) for oy in (-1, 0, 1))


def gp_col(gx, gy):
    return (gx & 1) + 2 * (gy & 1) + 4 * (gx >> 1) + 8 * (gy >> 1)


def par_col(px, py):
    return (px & 1) * 32 + (py & 1) * 16 + gp_col(px >> 1, py >> 1)


def leaf_col(x, y):
    return (x & 1) * 128 + (y & 1) * 64 + par_col(x >> 1, y >> 1)


def halo_cells(side):
    cells = []
    for dx, dy in DIRS:
        ex = -1 if dx < 0 else side
        ey = -1 if dy < 0 else side
        if dy == 0:
            cells.append([(ex, j) for j in range(side)])
        elif dx == 0:
            cells.append([(j, ey) for j in range(side)])
        else:
            cells.append([(ex, ey)])
    return cells


def pick_rows(side, col, base, lanes):
    out = np.zeros((HROWS, lanes), np.float32)
    for d, cells in enumerate(halo_cells(side)):
        for j, (cx, cy) in enumerate(cells):
            out[ROW_OF[d] + base[d] + j, col(cx % side, cy % side)] = 1.0
    return out


PAR_BASE = (0,) * 8
GP_BASE = (8,) * 4 + (1,) * 4


def shift_index(side, col, base, own_at, halo_at):
    where = {}
    for x in range(side):
        for y in range(side):
            where[x, y] = own_at + col(x, y)
    for d, cells in enumerate(halo_cells(side)):
        for j, cell in enumerate(cells):
            where[cell] = halo_at + ROW_OF[d] + base[d] + j
    out = np.zeros((9, side * side), np.int32)
    for o, (ox, oy) in enumerate(OFFS):
        for x in range(side):
            for y in range(side):
                out[o, col(x, y)] = where[x + ox, y + oy]
    return out


def cheb(u):
    terms = [u * 0 + 1.0, u]
    for _ in range(NODES - 2):
        terms.append(2.0 * u * terms[-1] - terms[-2])
    return terms


ANGLES = (2.0 * np.arange(NODES) + 1.0) * np.pi / (2.0 * NODES)
POINTS = np.cos(ANGLES)
S_COEF = 2.0 / NODES * np.cos(np.arange(NODES)[:, None] * ANGLES[None, :])
S_COEF[0] = 1.0 / NODES


def basis(u):
    terms = cheb(u)
    out = []
    for k in range(NODES):
        total = S_COEF[0, k] + float(S_COEF[1, k]) * terms[1]
        for n in range(2, NODES):
            total = total + float(S_COEF[n, k]) * terms[n]
        out.append(total)
    return out


def child_table():
    side = []
    for s in (0, 1):
        side.append(np.stack(basis(s - 0.5 + POINTS / 2), axis=1))
    out = np.zeros((4, NM, NM), np.float32)
    for sx in (0, 1):
        for sy in (0, 1):
            prod = side[sx][:, None, :, None] * side[sy][None, :, None, :]
            out[2 * sx + sy, :36, :36] = prod.reshape(36, 36)
    return out


def cell_vectors():
    coord = np.zeros((2, 4, NM), np.float32)
    cell = np.zeros((2, 4, NM), np.float32)
    for sx in (0, 1):
        for sy in (0, 1):
            ch = 2 * sx + sy
            node = np.arange(36)
            coord[0, ch] = sx - 0.5
            coord[1, ch] = sy - 0.5
            coord[0, ch, :36] += 0.5 * POINTS[node // 6]
            coord[1, ch, :36] += 0.5 * POINTS[node % 6]
            cell[0, ch] = sx
            cell[1, ch] = sy
    return coord.reshape(2, 4 * NM), cell.reshape(2, 4 * NM)


def constants():
    c = {}
    c["sel_leaf"] = pick_rows(LSIDE, leaf_col, PAR_BASE, 256).astype(BF16)
    sel_par = pick_rows(LSIDE // 2, par_col, PAR_BASE, 64)
    sel_gp = pick_rows(LSIDE // 4, gp_col, GP_BASE, 64)
    c["sel_mom"] = np.concatenate([sel_par, sel_gp], axis=1).astype(BF16)
    table = child_table()
    c["up"] = np.transpose(table, (2, 0, 1)).reshape(NM, 4 * NM)
    c["down"] = table.reshape(4 * NM, NM)
    src = np.zeros((16, 256), np.int32)
    src[:9] = shift_index(LSIDE, leaf_col, PAR_BASE, 0, 256)
    c["src_leaf"] = src
    msrc = np.full((16, 128), -1, np.int32)
    msrc[:9, :64] = shift_index(LSIDE // 2, par_col, PAR_BASE, 0, 128)
    msrc[:9, 64:80] = shift_index(LSIDE // 4, gp_col, GP_BASE, 64, 128)
    c["src_mom"] = msrc
    coord, cell = cell_vectors()
    rows = np.zeros((160, 128), np.float32)
    rows[:, 0:2] = coord.T
    rows[:, 2:4] = cell.T
    c["t_rows"] = rows
    cols = np.zeros((8, 9, 160), np.float32)
    for o, (ox, oy) in enumerate(OFFS):
        cols[0, o] = coord[0] + 2 * ox
        cols[1, o] = coord[1] + 2 * oy
        cols[2, o] = cell[0] + 2 * ox
        cols[3, o] = cell[1] + 2 * oy
    c["t_cols"] = cols.reshape(8, 1440)
    sides = np.zeros((8, HROWS), np.float32)
    for d, (dx, dy) in enumerate(DIRS):
        sides[0, ROW_OF[d] : ROW_OF[d] + ROWS_IN[d]] = dx
        sides[1, ROW_OF[d] : ROW_OF[d] + ROWS_IN[d]] = dy
    c["sides"] = sides
    return c


CONST = constants()


def split2(x):
    hi = x.astype(BF16)
    return hi, (x - hi.astype(F32)).astype(BF16)


def split3(x):
    hi = x.astype(BF16)
    rest = x - hi.astype(F32)
    mid = rest.astype(BF16)
    return hi, mid, (rest - mid.astype(F32)).astype(BF16)


def nt_dot(a, b):
    return lax.dot_general(a, b, (((1,), (1,)), ((), ())), preferred_element_type=F32)


def tn_none(a, b):
    return lax.dot_general(a, b, (((1,), (0,)), ((), ())), preferred_element_type=F32)


def prep_kernel(pos, mass, count, sel_leaf, sel_mom, up, own, mom, send, part, leaf_mom):
    starts = [qx * 2 + qy * 4 + sy for sy in (0, 1) for qx in (0, 1) for qy in (0, 1)]

    def rows_of(ref, lead, step):
        return jnp.concatenate(
            [ref[pl.ds(lead + step * s, 16, stride=8 * step), :] for s in starts], axis=0
        )

    u_rows = rows_of(pos, 0, 2)
    v_rows = rows_of(pos, 1, 2)
    m_rows = rows_of(mass, 0, 1)
    counts = rows_of(count, 0, 1)
    lane = lax.broadcasted_iota(jnp.int32, (128, 128), 1)
    live = (lane % PPL).astype(F32) < counts
    m_rows = jnp.where(live, m_rows, 0.0)
    l_rows = jnp.where(live, 1.0, 0.0)
    row = lax.broadcasted_iota(jnp.int32, (8, 128), 0)
    part[...] = jnp.where(
        row == 0,
        jnp.sum(m_rows, axis=0, keepdims=True),
        jnp.where(row == 1, jnp.sum(l_rows, axis=0, keepdims=True), 0.0),
    )
    for k, vals in enumerate((u_rows, v_rows, m_rows)):
        turned = vals.T
        own[k * PPL : (k + 1) * PPL, 0:128] = turned[:PPL]
        own[k * PPL : (k + 1) * PPL, 128:256] = turned[PPL:]
    leaf_mom[...] = jnp.zeros_like(leaf_mom)
    for tile in (0, 1):
        lanes = slice(tile * 128, tile * 128 + 128)
        bu = basis(own[0:64, lanes])
        bv = basis(own[64:128, lanes])
        m_t = own[128:192, lanes]
        live_t = jnp.where(m_t > 0.0, 1.0, 0.0)
        for kind, weight in enumerate((m_t, live_t)):
            for a in range(NODES):
                wa = bu[a] * weight
                for b in range(NODES):
                    leaf_mom[pl.ds(kind * NM + a * 6 + b, 1), lanes] = jnp.sum(
                        wa * bv[b], axis=0, keepdims=True
                    )
    mom[...] = jnp.zeros_like(mom)
    stacked = []
    for kind in (0, 1):
        block = jnp.concatenate(
            [
                leaf_mom[kind * NM : (kind + 1) * NM, ch * 64 : ch * 64 + 64]
                for ch in range(4)
            ],
            axis=0,
        )
        mom[kind * 160 : kind * 160 + 160, 0:64] = block
        stacked.append(block)
    par = jnp.dot(
        up[...], jnp.concatenate(stacked, axis=1), precision=HIGHEST, preferred_element_type=F32
    )
    for kind in (0, 1):
        for q in range(4):
            at = kind * 64 + q * 16
            mom[pl.ds(kind * 160 + q * NM, NM), 64:80] = par[:, at : at + 16]
    send[:, 0:192] = nt_dot(
        jnp.concatenate([sel_leaf[...]] * 3, axis=1),
        jnp.concatenate(split3(own[...]), axis=1),
    )
    send[:, 192:512] = nt_dot(
        jnp.concatenate([sel_mom[...]] * 3, axis=1),
        jnp.concatenate(split3(mom[...]), axis=1),
    )


def morton_split(code, bits):
    cx, cy = 0, 0
    for level in range((bits + 1) // 2):
        cx = cx + code // 4**level % 2 * 2**level
        cy = cy + code // (2 * 4**level) % 2 * 2**level
    return cx, cy


def morton_join(cx, cy, bits):
    code = 0
    for level in range((bits + 1) // 2):
        code = code + cx // 2**level % 2 * 4**level
        code = code + cy // 2**level % 2 * 2 * 4**level
    return code


def comm_kernel(dev_count, bits, send, part, recv, total, first, second, mid, sems_s, sems_r,
                sum_s1, sum_r1, sum_s2, sum_r2):
    code = lax.axis_index("grp") * dev_count + lax.axis_index("dev")
    bx, by = morton_split(code, bits)
    nx, ny = 2 ** ((bits + 1) // 2), 2 ** (bits // 2)
    low_n = 2 ** (bits // 2)
    high_n = 2**bits // low_n
    low, high = code % low_n, code // low_n

    def device(c):
        return {"grp": c // dev_count, "dev": c % dev_count}

    def beside(dx, dy):
        return device(morton_join((bx + dx + nx) % nx, (by + dy + ny) % ny, bits))

    barrier = pltpu.get_barrier_semaphore()
    for dx, dy in DIRS:
        pl.semaphore_signal(
            barrier, inc=1, device_id=beside(dx, dy), device_id_type=pl.DeviceIdType.MESH
        )

    def in_low(k):
        return device(high * low_n + (low + k) % low_n)

    def in_high(k):
        return device((high + k) % high_n * low_n + low)

    def greet_low(k, carry):
        pl.semaphore_signal(
            barrier, inc=1, device_id=in_low(k), device_id_type=pl.DeviceIdType.MESH
        )
        return carry

    def greet_high(k, carry):
        pl.semaphore_signal(
            barrier, inc=1, device_id=in_high(k), device_id_type=pl.DeviceIdType.MESH
        )
        return carry

    lax.fori_loop(1, low_n, greet_low, 0)
    lax.fori_loop(1, high_n, greet_high, 0)
    pl.semaphore_wait(barrier, 8 + low_n - 1 + high_n - 1)

    def low_copy(k):
        return pltpu.make_async_remote_copy(
            src_ref=part, dst_ref=first.at[k], send_sem=sum_s1.at[k], recv_sem=sum_r1.at[k],
            device_id=in_low(k), device_id_type=pl.DeviceIdType.MESH,
        )

    def high_copy(k):
        return pltpu.make_async_remote_copy(
            src_ref=mid, dst_ref=second.at[k], send_sem=sum_s2.at[k], recv_sem=sum_r2.at[k],
            device_id=in_high(k), device_id_type=pl.DeviceIdType.MESH,
        )

    def start_low(k, carry):
        low_copy(k).start()
        return carry

    def start_high(k, carry):
        high_copy(k).start()
        return carry

    lax.fori_loop(1, low_n, start_low, 0)
    edges = []
    for d, (dx, dy) in enumerate(DIRS):
        rows = pl.ds(ROW_OF[d], ROWS_IN[d])
        copy = pltpu.make_async_remote_copy(
            src_ref=send.at[rows], dst_ref=recv.at[rows], send_sem=sems_s.at[d],
            recv_sem=sems_r.at[d], device_id=beside(-dx, -dy),
            device_id_type=pl.DeviceIdType.MESH,
        )
        copy.start()
        edges.append(copy)

    def add_low(k, acc):
        low_copy(k).wait()
        return acc + first[k]

    def add_high(k, acc):
        high_copy(k).wait()
        return acc + second[k]

    mid[...] = lax.fori_loop(1, low_n, add_low, part[...])
    lax.fori_loop(1, high_n, start_high, 0)
    recv[96:HROWS, :] = jnp.zeros((HROWS - 96, LANES_OUT), F32)
    total[...] = lax.fori_loop(1, high_n, add_high, mid[...])
    for copy in edges:
        copy.wait()


def main_kernel(dev_count, bits, own, mom, recv, total, sides, src_leaf, src_mom, down, t_rows,
                t_cols, out, su, sv, sw, xs, table_hi, table_lo, leaf_local, result):
    code = lax.axis_index("grp") * dev_count + lax.axis_index("dev")
    bx, by = morton_split(code, bits)
    nx, ny = 2 ** ((bits + 1) // 2), 2 ** (bits // 2)
    sums = total[...]
    mass_sum = jnp.sum(sums[0:1], axis=1, keepdims=True)
    live_sum = jnp.sum(sums[1:2], axis=1, keepdims=True)
    mean = mass_sum / live_sum
    side_x = sides[0:1]
    side_y = sides[1:2]
    cell_x = side_x + jnp.full((1, 128), bx, jnp.int32).astype(F32)
    cell_y = side_y + jnp.full((1, 128), by, jnp.int32).astype(F32)
    inside = jnp.where(
        (cell_x >= 0.0) & (cell_x < float(nx)) & (cell_y >= 0.0) & (cell_y < float(ny)), 1.0, 0.0
    )
    halo = recv[...].T * inside

    both = jnp.concatenate([own[...], halo[0:192]], axis=1)
    m_all = both[128:192]
    weight = jnp.where(m_all > 0.0, m_all - mean, 0.0)
    sources = jnp.concatenate([both[0:128] * 0.5, weight], axis=0)
    cut = jnp.concatenate(split3(sources), axis=0)
    row384 = lax.broadcasted_iota(jnp.int32, (384, 256), 0)

    def shift_sources(o, carry):
        pick = jnp.where(row384 == src_leaf[pl.ds(o, 1), :], 1.0, 0.0).astype(BF16)
        moved = tn_none(cut, pick)
        moved = moved[0:192] + moved[192:384] + moved[384:576]
        off_x = (o // 3 - 1).astype(F32)
        off_y = (o % 3 - 1).astype(F32)
        at = pl.ds(pl.multiple_of(o * PPL, PPL), PPL)
        for tile in (0, 1):
            lanes = slice(tile * 128, tile * 128 + 128)
            su[tile, at, :] = moved[0:64, lanes] + off_x
            sv[tile, at, :] = moved[64:128, lanes] + off_y
            sw[tile, at, :] = moved[128:192, lanes]
        return carry

    lax.fori_loop(0, 9, shift_sources, 0)

    all_mom = jnp.concatenate([mom[...], halo[192:512]], axis=1)
    all_mom = all_mom[0:160] - mean * all_mom[160:320]
    cut_mom = jnp.concatenate(split2(all_mom), axis=0)
    row256 = lax.broadcasted_iota(jnp.int32, (256, 128), 0)

    def shift_moments(o, carry):
        pick = jnp.where(row256 == src_mom[pl.ds(o, 1), :], 1.0, 0.0).astype(BF16)
        moved = tn_none(cut_mom, pick).astype(BF16)
        at = pl.ds(pl.multiple_of(o * 160, 32), 160)
        xs[at, 0:128] = moved[0:160]
        xs[at, 128:256] = moved[160:320]
        return carry

    lax.fori_loop(0, 9, shift_moments, 0)

    def far(scale):
        def fill(i, carry):
            at = pl.multiple_of(i * 16, 16)
            rows = t_rows[pl.ds(at, 16), :]
            dx = (rows[:, 0:1] - t_cols[0:1, :]) * scale
            dy = (rows[:, 1:2] - t_cols[1:2, :]) * scale
            gap = jnp.maximum(
                jnp.abs(rows[:, 2:3] - t_cols[2:3, :]), jnp.abs(rows[:, 3:4] - t_cols[3:4, :])
            )
            x2 = dx * dx
            y2 = dy * dy
            inv = jnp.where(gap > 1.5, 1.0 / (x2 + y2 + SOFTEN), 0.0)
            inv_sq = inv * inv
            for c, val in enumerate(
                (dx * inv, dy * inv, (y2 - x2) * inv_sq, -2.0 * dx * dy * inv_sq)
            ):
                hi, lo = split2(val)
                table_hi[pl.ds(c * 160 + at, 16), :] = hi
                table_lo[pl.ds(c * 160 + at, 16), :] = lo
            return carry

        lax.fori_loop(0, 10, fill, 0)
        wide = tn_none(table_hi[...], xs[...])
        return wide[:, 0:128] + wide[:, 128:256] + tn_none(table_lo[...], xs[:, 0:128])

    par = far(2.0)
    par_cols = jnp.concatenate(
        [
            jnp.concatenate(
                [par[c * 160 + q * NM : c * 160 + q * NM + NM, 64:80] for q in range(4)], axis=1
            )
            for c in range(4)
        ],
        axis=1,
    )
    from_par = jnp.dot(
        down[...], par_cols, precision=HIGHEST, preferred_element_type=F32
    )
    leaf = far(1.0)
    for c in range(4):
        leaf_local[c] = jnp.concatenate(
            [
                leaf[c * 160 + ch * NM : c * 160 + ch * NM + NM, 0:64]
                + from_par[ch * NM : ch * NM + NM, c * 64 : c * 64 + 64]
                for ch in range(4)
            ],
            axis=1,
        )

    for tile in (0, 1):
        lanes = slice(tile * 128, tile * 128 + 128)
        bu = basis(own[0:64, lanes])
        bv = basis(own[64:128, lanes])
        for c in range(4):
            acc = None
            for a in range(NODES):
                half = leaf_local[c, pl.ds(a * 6, 1), lanes] * bv[0]
                for b in range(1, NODES):
                    half = half + leaf_local[c, pl.ds(a * 6 + b, 1), lanes] * bv[b]
                acc = half * bu[a] if acc is None else acc + half * bu[a]
            result[c, tile * PPL : tile * PPL + PPL, :] = acc

    width, unroll = 4, 4
    for tile in (0, 1):
        lanes = slice(tile * 128, tile * 128 + 128)
        for part in range(PPL // (8 * width)):
            base = part * 8 * width
            tx = [own[base + 8 * i : base + 8 * i + 8, lanes] * 0.5 for i in range(width)]
            ty = [own[64 + base + 8 * i : 72 + base + 8 * i, lanes] * 0.5 for i in range(width)]

            def pairs(step, acc):
                acc = list(acc)
                for i in range(unroll):
                    at = pl.ds(step * unroll + i, 8, stride=0)
                    sx, sy, w = su[tile, at, :], sv[tile, at, :], sw[tile, at, :]
                    for t in range(width):
                        dx = tx[t] - sx
                        dy = ty[t] - sy
                        x2 = dx * dx
                        y2 = dy * dy
                        inv = 1.0 / (x2 + y2 + SOFTEN)
                        w1 = w * inv
                        w2 = w1 * inv
                        acc[4 * t] = acc[4 * t] + w1 * dx
                        acc[4 * t + 1] = acc[4 * t + 1] + w1 * dy
                        acc[4 * t + 2] = acc[4 * t + 2] + w2 * (y2 - x2)
                        acc[4 * t + 3] = acc[4 * t + 3] + w2 * (dx * dy)
                return tuple(acc)

            zero = jnp.zeros((8, 128), F32)
            acc = lax.fori_loop(0, 9 * PPL // unroll, pairs, (zero,) * (4 * width))
            for t in range(width):
                rows = slice(tile * PPL + base + 8 * t, tile * PPL + base + 8 * t + 8)
                for c in range(4):
                    near = acc[4 * t + c]
                    if c == 3:
                        near = near * -2.0
                    result[c, rows, :] = result[c, rows, :] + near

    starts = [qx * 2 + qy * 4 + sy for sy in (0, 1) for qx in (0, 1) for qy in (0, 1)]
    for c in range(4):
        turned = result[c].T
        for i, s in enumerate(starts):
            out[pl.ds(s * 4 + c, 16, stride=32), :] = turned[16 * i : 16 * i + 16]


def vmem():
    return pl.BlockSpec(memory_space=pltpu.VMEM)


def on_device(particle_pos, particle_mass, leaf_counts):
    dev_count = lax.axis_size("dev")
    bits = (lax.axis_size("grp") * dev_count).bit_length() - 1
    low_n = 2 ** (bits // 2)
    high_n = 2**bits // low_n
    pos = particle_pos.reshape(2, 128, 128).transpose(1, 0, 2).reshape(256, 128)
    mass = particle_mass.reshape(128, 128)
    count = jnp.broadcast_to(
        leaf_counts.astype(F32).reshape(128, 2, 1), (128, 2, PPL)
    ).reshape(128, 128)
    c = {k: jnp.asarray(v) for k, v in CONST.items()}
    f32 = functools.partial(jax.ShapeDtypeStruct, dtype=F32)
    own, mom, send, part = pl.pallas_call(
        prep_kernel,
        out_shape=(f32((192, 256)), f32((320, 128)), f32((HROWS, LANES_OUT)), f32((8, 128))),
        in_specs=[vmem()] * 6,
        out_specs=(vmem(),) * 4,
        scratch_shapes=[pltpu.VMEM((2 * NM, 256), F32)],
        name="prep",
    )(pos, mass, count, c["sel_leaf"], c["sel_mom"], c["up"])
    recv, total = pl.pallas_call(
        functools.partial(comm_kernel, dev_count, bits),
        out_shape=(f32((HROWS, LANES_OUT)), f32((8, 128))),
        in_specs=[vmem()] * 2,
        out_specs=(vmem(),) * 2,
        scratch_shapes=[
            pltpu.VMEM((low_n, 8, 128), F32),
            pltpu.VMEM((high_n, 8, 128), F32),
            pltpu.VMEM((8, 128), F32),
            pltpu.SemaphoreType.DMA((8,)),
            pltpu.SemaphoreType.DMA((8,)),
            pltpu.SemaphoreType.DMA((low_n,)),
            pltpu.SemaphoreType.DMA((low_n,)),
            pltpu.SemaphoreType.DMA((high_n,)),
            pltpu.SemaphoreType.DMA((high_n,)),
        ],
        compiler_params=pltpu.CompilerParams(collective_id=0, has_side_effects=True),
        name="comm",
    )(send, part)
    out = pl.pallas_call(
        functools.partial(main_kernel, dev_count, bits),
        out_shape=f32((512, 128)),
        in_specs=[vmem()] * 10,
        out_specs=vmem(),
        scratch_shapes=[
            pltpu.VMEM((2, 9 * PPL, 128), F32),
            pltpu.VMEM((2, 9 * PPL, 128), F32),
            pltpu.VMEM((2, 9 * PPL, 128), F32),
            pltpu.VMEM((1440, 256), BF16),
            pltpu.VMEM((640, 1440), BF16),
            pltpu.VMEM((640, 1440), BF16),
            pltpu.VMEM((4, NM, 256), F32),
            pltpu.VMEM((4, 128, 128), F32),
        ],
        compiler_params=pltpu.CompilerParams(vmem_limit_bytes=48 * 2**20),
        name="fields",
    )(own, mom, recv, total, c["sides"], c["src_leaf"], c["src_mom"], c["down"], c["t_rows"],
      c["t_cols"])
    return out.reshape(128, 4, 128).transpose(1, 0, 2).reshape(4, LSIDE * LSIDE * PPL)


def solution(mesh):
    in_specs = (P(None, ("grp", "dev")), P(("grp", "dev")), P(("grp", "dev")))
    out_specs = P(None, ("grp", "dev"))
    return jax.shard_map(
        on_device, mesh=mesh, in_specs=in_specs, out_specs=out_specs, check_vma=False
    )
```

time: 537 us -> 75.3 us (0.14); the launches traced: 527 us -> 75.1 us
  local copies, waits for them, and re-layouts: 160 us -> 4.2 us
  other arithmetic: 145 us -> 0.01 us
  blocking collectives: 81.5 us -> 0 us
  Pallas kernels: 0 us -> 70.8 us
  loops' own time: 53.4 us -> 0 us
  matrix products: 37.4 us -> 0 us
  starting transfers between devices: 26.2 us -> 0 us
  waiting for transfers between devices: 17.6 us -> 0 us
  between operations: 5.99 us -> 0.11 us
    reshape x120 -> x1, local copies, waits for them, and re-layouts: 111 us -> 0.76 us  [on_device(): count = jnp.broadcast_to(leaf_counts.astype(F32).reshape(128, 2, 1), (128...]
    psum x1 -> x0, blocking collectives: 81.5 us -> none  [on_device(): lax.psum((jnp.sum(mass_rows * live_mask), jnp.sum(live_mask)), ('grp', 'd...]
    pallas_call x0 -> x3, Pallas kernels: none -> 70.8 us  [the longest x1 43.6 us: on_device(): pl.pallas_call(functools.partial(main_kernel, dev_count, bits), out_shape...]
    reduce_sum x18 -> x0, other arithmetic: 59.3 us -> none  [the longest x16 57.3 us: near_row(): jnp.sum(weight * term_val, axis=2)]
    another operation x1 -> x0, loops' own time: 53.4 us -> none  [on_device(): fields = lax.map(one_row, jnp.arange(LSIDE, dtype=jnp.int32))]
    another operation x50 -> x0, other arithmetic: 51.8 us -> none  [the longest x40 48.1 us: transfer_table(): stacked = jnp.stack([term_val for term_val in kernel_set])]
    dot_general x105 -> x0, matrix products: 37.4 us -> none  [the longest x80 24.8 us: far_field(): jnp.dot(transfer_table(half_width, off_x, off_y), shifted.reshape(NODES *...]
    ppermute x8 -> x0, starting transfers between devices: 26.2 us -> none  [partner(): return lax.ppermute(block, axis, route)]
  transfers between devices with their start and end apart: 8 -> 0, of which waited for: 5 -> 0; matrix products, arithmetic and copies ran while one was open for 36% -> 0% of each run, Pallas kernels for 0% -> 0%
where the time goes in v1:
time: 75.3 us; the launch traced here: 75.1 us
  Pallas kernels  70.8 us (94%)
  local copies, waits for them, and re-layouts  4.2 us (6%)
    pallas_call x1, Pallas kernels, on_device(): pl.pallas_call(functools.partial(main_kernel, dev_count, bits), out_shape...  43.6 us
    pallas_call x1, Pallas kernels, on_device(): pl.pallas_call(functools.partial(comm_kernel, dev_count, bits), out_shape...  23.9 us
    pallas_call x1, Pallas kernels, on_device(): pl.pallas_call(prep_kernel, out_shape=(f32((192, 256)), f32((320, 128)),...  3.26 us
    unnamed x22, local copies, waits for them, and re-layouts  3.25 us

profile of v1, /device:TPU:1, one launch (start us, length us, event | category | flops | bytes accessed | tf_op | source)
XLA Modules:
  0.0 75.1 jit_solution(8017931568083654059)
XLA Ops:
  0.0 0.0 copy-start.10
  0.0 0.7 copy-done.10
  0.7 0.1 broadcast_in_dim.7
  0.8 0.1 copy.16
  0.9 0.8 %copy.17.count = f32[128,128]{1,0:T(8,128)} copy(f32[128,128]{0,1:T(8,128)S(1)} %bitcast.12) | data formatting | bytes 131072 | tf_op jit(solution)/shard_map/reshape | solution.py:544
  1.7 0.0 copy-start.3
  1.7 0.0 copy-start.4
  1.7 3.3 %prep.1 = (f32[192,256]{1,0:T(8,128)}, f32[320,128]{1,0:T(8,128)}, f32[128,512]{1,0:T(8,128)}, f32[8,128]{1,0:T(8,128)}) custom-call(f32[256,128]{1,0:T(8,128)} %bitcast.13, f32[128,128]{1,0:T(8,128)} %bitcast.14, f32[128,128]{1,0:T(8,128)} %copy.17.count, bf16[128,256]{1,0:T(8,128)(2,1)} %constant.18.clone.sel_leaf, ...), custom_call_target="tpu_custom_call" | custom-call | tf_op jit(solution)/shard_map/prep/pallas_call | solution.py:547
  4.9 0.0 copy-start.1
  4.9 0.0 copy-start.5
  4.9 0.0 copy-start.6
  4.9 0.0 copy-start.7
  5.0 0.0 copy-start.8
  5.0 23.9 %comm.1 = (f32[128,512]{1,0:T(8,128)}, f32[8,128]{1,0:T(8,128)}) custom-call(f32[128,512]{1,0:T(8,128)} %get-tuple-element.13.send, f32[8,128]{1,0:T(8,128)} %get-tuple-element.14.part), custom_call_target="tpu_custom_call" | custom-call | tf_op jit(solution)/shard_map/comm/pallas_call | solution.py:555
  28.9 0.0 copy-done.3
  28.9 0.0 copy-done.4
  28.9 0.0 copy-done.1
  28.9 0.0 copy-done.5
  28.9 0.0 copy-done.6
  28.9 0.0 copy-done.7
  29.0 0.0 copy-done.8
  29.0 0.0 copy-start
  29.0 0.9 %copy-done = f32[128,512]{1,0:T(8,128)S(1)} copy-done((f32[128,512]{1,0:T(8,128)S(1)}, f32[128,512]{1,0:T(8,128)}, u32[]{:S(2)}) %copy-start) | copy-done | bytes 262168
  29.9 0.0 copy-start.2
  29.9 0.9 %copy-done.2 = f32[320,128]{1,0:T(8,128)S(1)} copy-done((f32[320,128]{1,0:T(8,128)S(1)}, f32[320,128]{1,0:T(8,128)}, u32[]{:S(2)}) %copy-start.2) | copy-done | bytes 163864
  30.8 0.0 copy-start.9
  30.8 0.7 copy-done.9
  31.5 43.6 %fields.1 = f32[512,128]{1,0:T(8,128)} custom-call(f32[192,256]{1,0:T(8,128)S(1)} %copy-done.1, f32[320,128]{1,0:T(8,128)S(1)} %copy-done.2, f32[128,512]{1,0:T(8,128)S(1)} %copy-done, f32[8,128]{1,0:T(8,128)S(1)} %copy-done.9, f32[8,128]{1,0:T(8,128)S(1)} %copy-done.8, s32[16,256]{1,0:T(8,128)S(1)} %copy-done.6, s32[16,128]{1,0:T(8,128)S(1)} %copy-done.7, ...), custom_call_target="tpu_custom_call" | custom-call | tf_op jit(solution)/shard_map/fields/pallas_call | solution.py:574
  (2 shorter events, 0.0 us)
Async XLA Ops:
  0.0 0.7 copy-start.10
  1.7 27.2 %copy-start.3 = (f32[160,128]{1,0:T(8,128)S(1)}, f32[160,128]{1,0:T(8,128)}, u32[]{:S(2)}) copy-start(f32[160,128]{1,0:T(8,128)} %constant.24.clone.t_rows) | copy-start | bytes 245764
  1.7 27.3 %copy-start.4 = (f32[160,40]{1,0:T(8,128)S(1)}, f32[160,40]{1,0:T(8,128)}, u32[]{:S(2)}) copy-start(f32[160,40]{1,0:T(8,128)} %constant.21.clone.down) | copy-start | bytes 76804
  4.9 24.0 %copy-start.1 = (f32[192,256]{1,0:T(8,128)S(1)}, f32[192,256]{1,0:T(8,128)}, u32[]{:S(2)}) copy-start(f32[192,256]{1,0:T(8,128)} %get-tuple-element.11.own) | copy-start | bytes 589828
  4.9 24.0 %copy-start.5 = (f32[8,1440]{1,0:T(8,128)S(1)}, f32[8,1440]{1,0:T(8,128)}, u32[]{:S(2)}) copy-start(f32[8,1440]{1,0:T(8,128)} %constant.25.clone.t_cols) | copy-start | bytes 138244
  4.9 24.0 %copy-start.6 = (s32[16,256]{1,0:T(8,128)S(1)}, s32[16,256]{1,0:T(8,128)}, u32[]{:S(2)}) copy-start(s32[16,256]{1,0:T(8,128)} %constant.22.clone.src_leaf) | copy-start | bytes 49156
  4.9 24.0 %copy-start.7 = (s32[16,128]{1,0:T(8,128)S(1)}, s32[16,128]{1,0:T(8,128)}, u32[]{:S(2)}) copy-start(s32[16,128]{1,0:T(8,128)} %constant.23.clone.src_mom) | copy-start | bytes 24580
  5.0 24.0 %copy-start.8 = (f32[8,128]{1,0:T(8,128)S(1)}, f32[8,128]{1,0:T(8,128)}, u32[]{:S(2)}) copy-start(f32[8,128]{1,0:T(8,128)} %constant.26.clone.sides) | copy-start | bytes 12292
  29.0 1.0 %copy-start = (f32[128,512]{1,0:T(8,128)S(1)}, f32[128,512]{1,0:T(8,128)}, u32[]{:S(2)}) copy-start(f32[128,512]{1,0:T(8,128)} %get-tuple-element.15.recv) | copy-start | bytes 786436
  29.9 0.9 %copy-start.2 = (f32[320,128]{1,0:T(8,128)S(1)}, f32[320,128]{1,0:T(8,128)}, u32[]{:S(2)}) copy-start(f32[320,128]{1,0:T(8,128)} %get-tuple-element.12.mom) | copy-start | bytes 491524
  30.8 0.7 copy-start.9

commit v2 on v1

v2 whole, which is shorter than its diff:
```python
import functools

import jax
import jax.numpy as jnp
import numpy as np
from jax import lax
from jax.experimental import pallas as pl
from jax.experimental.pallas import tpu as pltpu
from jax.sharding import PartitionSpec as P

NODES = 6
PPL = 64
LSIDE = 16
SOFTEN = 0.01
NM = 40
HIGHEST = lax.Precision.HIGHEST
F32 = jnp.float32
BF16 = jnp.bfloat16

DIRS = ((-1, 0), (1, 0), (0, -1), (0, 1), (-1, -1), (1, -1), (-1, 1), (1, 1))
ROW_OF = (0, 16, 32, 48, 64, 72, 80, 88)
ROWS_IN = (16, 16, 16, 16, 8, 8, 8, 8)
HROWS = 128
LANES_OUT = 512
OFFS = tuple((ox, oy) for ox in (-1, 0, 1) for oy in (-1, 0, 1) if (ox, oy) != (0, 0)) + ((0, 0),)
NEIGHBOURS = 8


def gp_col(gx, gy):
    return (gx & 1) + 2 * (gy & 1) + 4 * (gx >> 1) + 8 * (gy >> 1)


def par_col(px, py):
    return (px & 1) * 32 + (py & 1) * 16 + gp_col(px >> 1, py >> 1)


def leaf_col(x, y):
    return (x & 1) * 128 + (y & 1) * 64 + par_col(x >> 1, y >> 1)


def halo_cells(side):
    cells = []
    for dx, dy in DIRS:
        ex = -1 if dx < 0 else side
        ey = -1 if dy < 0 else side
        if dy == 0:
            cells.append([(ex, j) for j in range(side)])
        elif dx == 0:
            cells.append([(j, ey) for j in range(side)])
        else:
            cells.append([(ex, ey)])
    return cells


def pick_rows(side, col, base, lanes):
    out = np.zeros((HROWS, lanes), np.float32)
    for d, cells in enumerate(halo_cells(side)):
        for j, (cx, cy) in enumerate(cells):
            out[ROW_OF[d] + base[d] + j, col(cx % side, cy % side)] = 1.0
    return out


PAR_BASE = (0,) * 8
GP_BASE = (8,) * 4 + (1,) * 4


def shift_index(side, col, base, own_at, halo_at):
    where = {}
    for x in range(side):
        for y in range(side):
            where[x, y] = own_at + col(x, y)
    for d, cells in enumerate(halo_cells(side)):
        for j, cell in enumerate(cells):
            where[cell] = halo_at + ROW_OF[d] + base[d] + j
    out = np.zeros((9, side * side), np.int32)
    for o, (ox, oy) in enumerate(OFFS):
        for x in range(side):
            for y in range(side):
                out[o, col(x, y)] = where[x + ox, y + oy]
    return out


def cheb(u):
    terms = [u * 0 + 1.0, u]
    for _ in range(NODES - 2):
        terms.append(2.0 * u * terms[-1] - terms[-2])
    return terms


ANGLES = (2.0 * np.arange(NODES) + 1.0) * np.pi / (2.0 * NODES)
POINTS = np.cos(ANGLES)
S_COEF = 2.0 / NODES * np.cos(np.arange(NODES)[:, None] * ANGLES[None, :])
S_COEF[0] = 1.0 / NODES


def basis(u):
    terms = cheb(u)
    out = []
    for k in range(NODES):
        total = S_COEF[0, k] + float(S_COEF[1, k]) * terms[1]
        for n in range(2, NODES):
            total = total + float(S_COEF[n, k]) * terms[n]
        out.append(total)
    return out


def child_table():
    side = []
    for s in (0, 1):
        side.append(np.stack(basis(s - 0.5 + POINTS / 2), axis=1))
    out = np.zeros((4, NM, NM), np.float32)
    for sx in (0, 1):
        for sy in (0, 1):
            prod = side[sx][:, None, :, None] * side[sy][None, :, None, :]
            out[2 * sx + sy, :36, :36] = prod.reshape(36, 36)
    return out


def cell_vectors():
    coord = np.zeros((2, 4, NM), np.float32)
    cell = np.zeros((2, 4, NM), np.float32)
    for sx in (0, 1):
        for sy in (0, 1):
            ch = 2 * sx + sy
            node = np.arange(36)
            coord[0, ch] = sx - 0.5
            coord[1, ch] = sy - 0.5
            coord[0, ch, :36] += 0.5 * POINTS[node // 6]
            coord[1, ch, :36] += 0.5 * POINTS[node % 6]
            cell[0, ch] = sx
            cell[1, ch] = sy
    return coord.reshape(2, 4 * NM), cell.reshape(2, 4 * NM)


def constants():
    c = {}
    c["sel_leaf"] = pick_rows(LSIDE, leaf_col, PAR_BASE, 256).astype(BF16)
    sel_par = pick_rows(LSIDE // 2, par_col, PAR_BASE, 64)
    sel_gp = pick_rows(LSIDE // 4, gp_col, GP_BASE, 64)
    c["sel_mom"] = np.concatenate([sel_par, sel_gp], axis=1).astype(BF16)
    table = child_table()
    c["up"] = np.transpose(table, (2, 0, 1)).reshape(NM, 4 * NM)
    c["down"] = table.reshape(4 * NM, NM)
    src = np.zeros((16, 256), np.int32)
    src[:9] = shift_index(LSIDE, leaf_col, PAR_BASE, 0, 256)
    for x in range(LSIDE):
        for y in range(LSIDE):
            src[9, leaf_col(x, y)] = sum(
                (x >> k & 1) << 2 * k | (y >> k & 1) << 2 * k + 1 for k in range(4)
            )
    c["src_leaf"] = src
    msrc = np.full((16, 128), -1, np.int32)
    msrc[:9, :64] = shift_index(LSIDE // 2, par_col, PAR_BASE, 0, 128)
    msrc[:9, 64:80] = shift_index(LSIDE // 4, gp_col, GP_BASE, 64, 128)
    c["src_mom"] = msrc
    coord, cell = cell_vectors()
    rows = np.zeros((160, 128), np.float32)
    rows[:, 0:2] = coord.T
    rows[:, 2:4] = cell.T
    c["t_rows"] = rows
    cols = np.zeros((8, 9, 160), np.float32)
    for o, (ox, oy) in enumerate(OFFS):
        cols[0, o] = coord[0] + 2 * ox
        cols[1, o] = coord[1] + 2 * oy
        cols[2, o] = cell[0] + 2 * ox
        cols[3, o] = cell[1] + 2 * oy
    c["t_cols"] = cols.reshape(8, 1440)
    sides = np.zeros((8, HROWS), np.float32)
    for d, (dx, dy) in enumerate(DIRS):
        sides[0, ROW_OF[d] : ROW_OF[d] + ROWS_IN[d]] = dx
        sides[1, ROW_OF[d] : ROW_OF[d] + ROWS_IN[d]] = dy
    c["sides"] = sides
    return c


CONST = constants()


def split2(x):
    hi = x.astype(BF16)
    return hi, (x - hi.astype(F32)).astype(BF16)


def split3(x):
    hi = x.astype(BF16)
    rest = x - hi.astype(F32)
    mid = rest.astype(BF16)
    return hi, mid, (rest - mid.astype(F32)).astype(BF16)


def nt_dot(a, b):
    return lax.dot_general(a, b, (((1,), (1,)), ((), ())), preferred_element_type=F32)


def tn_none(a, b):
    return lax.dot_general(a, b, (((1,), (0,)), ((), ())), preferred_element_type=F32)


def morton_split(code, bits):
    cx, cy = 0, 0
    for level in range((bits + 1) // 2):
        cx = cx + code // 4**level % 2 * 2**level
        cy = cy + code // (2 * 4**level) % 2 * 2**level
    return cx, cy


def morton_join(cx, cy, bits):
    code = 0
    for level in range((bits + 1) // 2):
        code = code + cx // 2**level % 2 * 4**level
        code = code + cy // 2**level % 2 * 2 * 4**level
    return code


def whole_kernel(dev_count, bits, *refs):
    sources, refs = refs[:OPERANDS], refs[OPERANDS:]
    out, refs = refs[0], refs[1:]
    held, refs = refs[:OPERANDS], refs[OPERANDS:]
    (pos, mass, count, src_leaf, sel_leaf, sel_mom, up, t_rows, t_cols, sides, src_mom,
     down) = held
    arrive_sems = refs[0]
    arrivals = [
        pltpu.make_async_copy(src, dst, arrive_sems.at[i])
        for i, (src, dst) in enumerate(zip(sources, held))
    ]
    for arrival in arrivals:
        arrival.start()
    run_kernel(dev_count, bits, arrivals, pos, mass, count, sel_leaf, sel_mom, up, down, sides,
               src_leaf, src_mom, t_rows, t_cols, out, *refs[1:])


def run_kernel(dev_count, bits, arrivals, pos, mass, count, sel_leaf, sel_mom, up, down, sides,
               src_leaf, src_mom, t_rows, t_cols, out, own, mom, send, recv, part, mid, leaf_mom, first,
                 second, su, sv, sw, lone, xs, hi_leaf, lo_leaf, hi_par, lo_par, leaf_local,
                 result, self_live, edge_s, edge_r, sum_s1, sum_r1, sum_s2, sum_r2):
    code = lax.axis_index("grp") * dev_count + lax.axis_index("dev")
    bx, by = morton_split(code, bits)
    nx, ny = 2 ** ((bits + 1) // 2), 2 ** (bits // 2)
    low_n = 2 ** (bits // 2)
    high_n = 2**bits // low_n
    low, high = code % low_n, code // low_n

    def device(c):
        return {"grp": c // dev_count, "dev": c % dev_count}

    def beside(dx, dy):
        return device(morton_join((bx + dx + nx) % nx, (by + dy + ny) % ny, bits))

    def in_low(k):
        return device(high * low_n + (low + k) % low_n)

    def in_high(k):
        return device((high + k) % high_n * low_n + low)

    barrier = pltpu.get_barrier_semaphore()

    def greet(who):
        pl.semaphore_signal(barrier, inc=1, device_id=who, device_id_type=pl.DeviceIdType.MESH)

    def greet_low(k, carry):
        greet(in_low(k))
        return carry

    def greet_high(k, carry):
        greet(in_high(k))
        return carry

    lax.fori_loop(1, low_n, greet_low, 0)
    for dx, dy in DIRS:
        greet(beside(dx, dy))
    lax.fori_loop(1, high_n, greet_high, 0)

    starts = [qx * 2 + qy * 4 + sy for sy in (0, 1) for qx in (0, 1) for qy in (0, 1)]

    def turned(ref, lead, step):
        rows = jnp.concatenate(
            [ref[pl.ds(lead + step * s, 16, stride=8 * step), :] for s in starts], axis=0
        )
        return rows.T

    for arrival in arrivals[:4]:
        arrival.wait()
    row256 = lax.broadcasted_iota(jnp.int32, (256, 256), 0)
    pick = jnp.where(row256 == src_leaf[9:10, :], 1.0, 0.0).astype(BF16)
    linear = count[...].astype(F32).astype(BF16)
    counts = tn_none(linear[0:1], pick[0:128]) + tn_none(linear[1:2], pick[128:256])
    m_turned = turned(mass, 0, 1)
    slot = lax.broadcasted_iota(jnp.int32, (PPL, 128), 0).astype(F32)
    totals = []
    for tile in (0, 1):
        lanes = slice(tile * 128, tile * 128 + 128)
        live = slot < counts[:, lanes]
        vals = jnp.where(live, m_turned[tile * PPL : tile * PPL + PPL], 0.0)
        own[128:192, lanes] = vals
        totals.append(jnp.sum(vals, axis=0, keepdims=True))
    row = lax.broadcasted_iota(jnp.int32, (8, 128), 0)
    part[...] = jnp.where(
        row == 0,
        totals[0] + totals[1],
        jnp.where(row == 1, counts[:, 0:128] + counts[:, 128:256], 0.0),
    )
    for k in (0, 1):
        vals = turned(pos, k, 2)
        own[k * PPL : (k + 1) * PPL, 0:128] = vals[:PPL]
        own[k * PPL : (k + 1) * PPL, 128:256] = vals[PPL:]

    def low_copy(k):
        return pltpu.make_async_remote_copy(
            src_ref=part, dst_ref=first.at[k], send_sem=sum_s1.at[k], recv_sem=sum_r1.at[k],
            device_id=in_low(k), device_id_type=pl.DeviceIdType.MESH,
        )

    def high_copy(k):
        return pltpu.make_async_remote_copy(
            src_ref=mid, dst_ref=second.at[k], send_sem=sum_s2.at[k], recv_sem=sum_r2.at[k],
            device_id=in_high(k), device_id_type=pl.DeviceIdType.MESH,
        )

    def start_low(k, carry):
        low_copy(k).start()
        return carry

    def start_high(k, carry):
        high_copy(k).start()
        return carry

    def add_low(k, acc):
        low_copy(k).wait()
        return acc + first[k]

    def add_high(k, acc):
        high_copy(k).wait()
        return acc + second[k]

    pl.semaphore_wait(barrier, 8 + low_n - 1 + high_n - 1)
    lax.fori_loop(1, low_n, start_low, 0)

    for arrival in arrivals[4:]:
        arrival.wait()
    leaf_mom[...] = jnp.zeros_like(leaf_mom)
    for tile in (0, 1):
        lanes = slice(tile * 128, tile * 128 + 128)
        bu = basis(own[0:64, lanes])
        bv = basis(own[64:128, lanes])
        m_t = own[128:192, lanes]
        live_t = jnp.where(m_t > 0.0, 1.0, 0.0)
        lone[tile, 0:PPL, :] = live_t
        for kind, weight in enumerate((m_t, live_t)):
            for a in range(NODES):
                wa = bu[a] * weight
                for b in range(NODES):
                    leaf_mom[pl.ds(kind * NM + a * 6 + b, 1), lanes] = jnp.sum(
                        wa * bv[b], axis=0, keepdims=True
                    )
    mom[...] = jnp.zeros_like(mom)
    stacked = []
    for kind in (0, 1):
        block = jnp.concatenate(
            [
                leaf_mom[kind * NM : (kind + 1) * NM, ch * 64 : ch * 64 + 64]
                for ch in range(4)
            ],
            axis=0,
        )
        mom[kind * 160 : kind * 160 + 160, 0:64] = block
        stacked.append(block)
    par = jnp.dot(
        up[...], jnp.concatenate(stacked, axis=1), precision=HIGHEST, preferred_element_type=F32
    )
    for kind in (0, 1):
        for q in range(4):
            at = kind * 64 + q * 16
            mom[pl.ds(kind * 160 + q * NM, NM), 64:80] = par[:, at : at + 16]
    own_cut = split3(own[...])
    send[:, 0:192] = nt_dot(
        jnp.concatenate([sel_leaf[...]] * 3, axis=1), jnp.concatenate(own_cut, axis=1)
    )
    send[:, 192:512] = nt_dot(
        jnp.concatenate([sel_mom[...]] * 3, axis=1),
        jnp.concatenate(split3(mom[...]), axis=1),
    )
    edges = []
    for d, (dx, dy) in enumerate(DIRS):
        rows = pl.ds(ROW_OF[d], ROWS_IN[d])
        copy = pltpu.make_async_remote_copy(
            src_ref=send.at[rows], dst_ref=recv.at[rows], send_sem=edge_s.at[d],
            recv_sem=edge_r.at[d], device_id=beside(-dx, -dy),
            device_id_type=pl.DeviceIdType.MESH,
        )
        copy.start()
        edges.append(copy)
    recv[96:HROWS, :] = jnp.zeros((HROWS - 96, LANES_OUT), F32)

    def fill_tables(scale, table_hi, table_lo):
        def fill(i, carry):
            at = pl.multiple_of(i * 16, 16)
            rows = t_rows[pl.ds(at, 16), :]
            dx = (rows[:, 0:1] - t_cols[0:1, :]) * scale
            dy = (rows[:, 1:2] - t_cols[1:2, :]) * scale
            gap = jnp.maximum(
                jnp.abs(rows[:, 2:3] - t_cols[2:3, :]), jnp.abs(rows[:, 3:4] - t_cols[3:4, :])
            )
            x2 = dx * dx
            y2 = dy * dy
            inv = jnp.where(gap > 1.5, 1.0 / (x2 + y2 + SOFTEN), 0.0)
            inv_sq = inv * inv
            for c, val in enumerate(
                (dx * inv, dy * inv, (y2 - x2) * inv_sq, -2.0 * dx * dy * inv_sq)
            ):
                hi, lo = split2(val)
                table_hi[pl.ds(c * 160 + at, 16), :] = hi
                table_lo[pl.ds(c * 160 + at, 16), :] = lo
            return carry

        lax.fori_loop(0, 10, fill, 0)

    fill_tables(2.0, hi_par, lo_par)
    mid[...] = lax.fori_loop(1, low_n, add_low, part[...])
    lax.fori_loop(1, high_n, start_high, 0)
    fill_tables(1.0, hi_leaf, lo_leaf)

    def at_offset(o):
        return pl.ds(pl.multiple_of(o * PPL, PPL), PPL)

    own_rows = jnp.concatenate(own_cut, axis=0)

    def shift_own(o, carry):
        hot = jnp.where(row256 == src_leaf[pl.ds(o, 1), :], 1.0, 0.0).astype(BF16)
        moved = tn_none(own_rows, hot)
        moved = moved[0:192] + moved[192:384] + moved[384:576]
        for tile in (0, 1):
            lanes = slice(tile * 128, tile * 128 + 128)
            su[tile, at_offset(o), :] = moved[0:64, lanes]
            sv[tile, at_offset(o), :] = moved[64:128, lanes]
            sw[tile, at_offset(o), :] = moved[128:192, lanes]
        return carry

    lax.fori_loop(0, NEIGHBOURS, shift_own, 0)
    self_at = NEIGHBOURS * PPL
    for tile in (0, 1):
        lanes = slice(tile * 128, tile * 128 + 128)
        su[tile, self_at : self_at + PPL, :] = own[0:64, lanes] * 0.5
        sv[tile, self_at : self_at + PPL, :] = own[64:128, lanes] * 0.5
        sw[tile, self_at : self_at + PPL, :] = own[128:192, lanes]

    zero = jnp.zeros((8, 128), F32)

    def targets(tile, base, width):
        lanes = slice(tile * 128, tile * 128 + 128)
        tx = [own[base + 8 * i : base + 8 * i + 8, lanes] * 0.5 for i in range(width)]
        ty = [own[64 + base + 8 * i : 72 + base + 8 * i, lanes] * 0.5 for i in range(width)]
        return tx, ty

    self_width = 2
    for tile in (0, 1):
        for piece in range(PPL // (8 * self_width)):
            base = piece * 8 * self_width
            tx, ty = targets(tile, base, self_width)

            def self_pairs(step, acc, tile=tile, tx=tx, ty=ty):
                acc = list(acc)
                for i in range(4):
                    k = step * 4 + i
                    at = pl.ds(self_at + k, 8, stride=0)
                    sx, sy, m = su[tile, at, :], sv[tile, at, :], sw[tile, at, :]
                    one = lone[tile, pl.ds(k, 8, stride=0), :]
                    for t in range(self_width):
                        dx = tx[t] - sx
                        dy = ty[t] - sy
                        x2 = dx * dx
                        y2 = dy * dy
                        inv = 1.0 / (x2 + y2 + SOFTEN)
                        gap = y2 - x2
                        cross = dx * dy
                        for kind, w in enumerate((m, one)):
                            at_acc = 8 * t + 4 * kind
                            w1 = w * inv
                            w2 = w1 * inv
                            acc[at_acc] = acc[at_acc] + w1 * dx
                            acc[at_acc + 1] = acc[at_acc + 1] + w1 * dy
                            acc[at_acc + 2] = acc[at_acc + 2] + w2 * gap
                            acc[at_acc + 3] = acc[at_acc + 3] + w2 * cross
                return tuple(acc)

            acc = lax.fori_loop(0, PPL // 4, self_pairs, (zero,) * (8 * self_width))
            for t in range(self_width):
                rows = slice(tile * PPL + base + 8 * t, tile * PPL + base + 8 * t + 8)
                for c in range(4):
                    scale = -2.0 if c == 3 else 1.0
                    result[c, rows, :] = acc[8 * t + c] * scale
                    self_live[c, rows, :] = acc[8 * t + 4 + c] * scale

    sums = lax.fori_loop(1, high_n, add_high, mid[...])
    mass_sum = jnp.sum(sums[0:1], axis=1, keepdims=True)
    live_sum = jnp.sum(sums[1:2], axis=1, keepdims=True)
    mean = mass_sum / live_sum
    for copy in edges:
        copy.wait()
    cell_x = sides[0:1] + jnp.full((1, 128), bx, jnp.int32).astype(F32)
    cell_y = sides[1:2] + jnp.full((1, 128), by, jnp.int32).astype(F32)
    inside = jnp.where(
        (cell_x >= 0.0) & (cell_x < float(nx)) & (cell_y >= 0.0) & (cell_y < float(ny)), 1.0, 0.0
    )
    halo = recv[...].T * inside
    halo_rows = jnp.concatenate(split3(halo[0:192]), axis=0)
    row128 = lax.broadcasted_iota(jnp.int32, (128, 256), 0) + 256

    def shift_halo(o, carry):
        hot = jnp.where(row128 == src_leaf[pl.ds(o, 1), :], 1.0, 0.0).astype(BF16)
        moved = tn_none(halo_rows, hot)
        moved = moved[0:192] + moved[192:384] + moved[384:576]
        skip = o + (o >= 4).astype(jnp.int32)
        off_x = (skip // 3 - 1).astype(F32)
        off_y = (skip % 3 - 1).astype(F32)
        for tile in (0, 1):
            lanes = slice(tile * 128, tile * 128 + 128)
            at = at_offset(o)
            su[tile, at, :] = (su[tile, at, :] + moved[0:64, lanes]) * 0.5 + off_x
            sv[tile, at, :] = (sv[tile, at, :] + moved[64:128, lanes]) * 0.5 + off_y
            m = sw[tile, at, :] + moved[128:192, lanes]
            sw[tile, at, :] = jnp.where(m > 0.0, m - mean, 0.0)
        return carry

    lax.fori_loop(0, NEIGHBOURS, shift_halo, 0)

    all_mom = jnp.concatenate([mom[...], halo[192:512]], axis=1)
    all_mom = all_mom[0:160] - mean * all_mom[160:320]
    cut_mom = jnp.concatenate(split2(all_mom), axis=0)

    def shift_moments(o, carry):
        hot = jnp.where(row256[:, 0:128] == src_mom[pl.ds(o, 1), :], 1.0, 0.0).astype(BF16)
        moved = tn_none(cut_mom, hot).astype(BF16)
        at = pl.ds(pl.multiple_of(o * 160, 32), 160)
        xs[at, 0:128] = moved[0:160]
        xs[at, 128:256] = moved[160:320]
        return carry

    lax.fori_loop(0, 9, shift_moments, 0)

    def far(table_hi, table_lo):
        wide = tn_none(table_hi[...], xs[...])
        return wide[:, 0:128] + wide[:, 128:256] + tn_none(table_lo[...], xs[:, 0:128])

    par = far(hi_par, lo_par)
    par_cols = jnp.concatenate(
        [
            jnp.concatenate(
                [par[c * 160 + q * NM : c * 160 + q * NM + NM, 64:80] for q in range(4)], axis=1
            )
            for c in range(4)
        ],
        axis=1,
    )
    from_par = jnp.dot(
        down[...], par_cols, precision=HIGHEST, preferred_element_type=F32
    )
    leaf = far(hi_leaf, lo_leaf)
    for c in range(4):
        leaf_local[c] = jnp.concatenate(
            [
                leaf[c * 160 + ch * NM : c * 160 + ch * NM + NM, 0:64]
                + from_par[ch * NM : ch * NM + NM, c * 64 : c * 64 + 64]
                for ch in range(4)
            ],
            axis=1,
        )

    for tile in (0, 1):
        lanes = slice(tile * 128, tile * 128 + 128)
        bu = basis(own[0:64, lanes])
        bv = basis(own[64:128, lanes])
        for c in range(4):
            rows = slice(tile * PPL, tile * PPL + PPL)
            acc = result[c, rows, :] - mean * self_live[c, rows, :]
            for a in range(NODES):
                half = leaf_local[c, pl.ds(a * 6, 1), lanes] * bv[0]
                for b in range(1, NODES):
                    half = half + leaf_local[c, pl.ds(a * 6 + b, 1), lanes] * bv[b]
                acc = acc + half * bu[a]
            result[c, rows, :] = acc

    width, unroll = 4, 8
    for tile in (0, 1):
        for piece in range(PPL // (8 * width)):
            base = piece * 8 * width
            tx, ty = targets(tile, base, width)

            def pairs(step, acc, tile=tile, tx=tx, ty=ty):
                acc = list(acc)
                for i in range(unroll):
                    at = pl.ds(step * unroll + i, 8, stride=0)
                    sx, sy, w = su[tile, at, :], sv[tile, at, :], sw[tile, at, :]
                    for t in range(width):
                        dx = tx[t] - sx
                        dy = ty[t] - sy
                        x2 = dx * dx
                        y2 = dy * dy
                        inv = 1.0 / (x2 + y2 + SOFTEN)
                        w1 = w * inv
                        w2 = w1 * inv
                        acc[4 * t] = acc[4 * t] + w1 * dx
                        acc[4 * t + 1] = acc[4 * t + 1] + w1 * dy
                        acc[4 * t + 2] = acc[4 * t + 2] + w2 * (y2 - x2)
                        acc[4 * t + 3] = acc[4 * t + 3] + w2 * (dx * dy)
                return tuple(acc)

            acc = lax.fori_loop(0, NEIGHBOURS * PPL // unroll, pairs, (zero,) * (4 * width))
            for t in range(width):
                rows = slice(tile * PPL + base + 8 * t, tile * PPL + base + 8 * t + 8)
                for c in range(4):
                    near = acc[4 * t + c]
                    if c == 3:
                        near = near * -2.0
                    result[c, rows, :] = result[c, rows, :] + near

    for c in range(4):
        back = result[c].T
        for i, s in enumerate(starts):
            out[pl.ds(s * 4 + c, 16, stride=32), :] = back[16 * i : 16 * i + 16]


def vmem():
    return pl.BlockSpec(memory_space=pltpu.VMEM)


NAMES = ("src_leaf", "sel_leaf", "sel_mom", "up", "t_rows", "t_cols", "sides", "src_mom", "down")
OPERANDS = 3 + len(NAMES)


def on_device(particle_pos, particle_mass, leaf_counts):
    dev_count = lax.axis_size("dev")
    bits = (lax.axis_size("grp") * dev_count).bit_length() - 1
    low_n = 2 ** (bits // 2)
    high_n = 2**bits // low_n
    pos = particle_pos.reshape(2, 128, 128).transpose(1, 0, 2).reshape(256, 128)
    mass = particle_mass.reshape(128, 128)
    count = leaf_counts.reshape(2, 128)
    operands = (pos, mass, count, *[jnp.asarray(CONST[k]) for k in NAMES])
    out = pl.pallas_call(
        functools.partial(whole_kernel, dev_count, bits),
        out_shape=jax.ShapeDtypeStruct((512, 128), F32),
        in_specs=[pl.BlockSpec(memory_space=pltpu.HBM)] * OPERANDS,
        out_specs=vmem(),
        scratch_shapes=[pltpu.VMEM(x.shape, x.dtype) for x in operands]
        + [
            pltpu.SemaphoreType.DMA((OPERANDS,)),
            pltpu.VMEM((192, 256), F32),
            pltpu.VMEM((320, 128), F32),
            pltpu.VMEM((HROWS, LANES_OUT), F32),
            pltpu.VMEM((HROWS, LANES_OUT), F32),
            pltpu.VMEM((8, 128), F32),
            pltpu.VMEM((8, 128), F32),
            pltpu.VMEM((2 * NM, 256), F32),
            pltpu.VMEM((low_n, 8, 128), F32),
            pltpu.VMEM((high_n, 8, 128), F32),
            pltpu.VMEM((2, 9 * PPL + 8, 128), F32),
            pltpu.VMEM((2, 9 * PPL + 8, 128), F32),
            pltpu.VMEM((2, 9 * PPL + 8, 128), F32),
            pltpu.VMEM((2, PPL + 8, 128), F32),
            pltpu.VMEM((1440, 256), BF16),
            pltpu.VMEM((640, 1440), BF16),
            pltpu.VMEM((640, 1440), BF16),
            pltpu.VMEM((640, 1440), BF16),
            pltpu.VMEM((640, 1440), BF16),
            pltpu.VMEM((4, NM, 256), F32),
            pltpu.VMEM((4, 128, 128), F32),
            pltpu.VMEM((4, 128, 128), F32),
            pltpu.SemaphoreType.DMA((8,)),
            pltpu.SemaphoreType.DMA((8,)),
            pltpu.SemaphoreType.DMA((low_n,)),
            pltpu.SemaphoreType.DMA((low_n,)),
            pltpu.SemaphoreType.DMA((high_n,)),
            pltpu.SemaphoreType.DMA((high_n,)),
        ],
        compiler_params=pltpu.CompilerParams(
            collective_id=0, has_side_effects=True, vmem_limit_bytes=63 * 2**20
        ),
        name="fields",
    )(*operands)
    return out.reshape(128, 4, 128).transpose(1, 0, 2).reshape(4, LSIDE * LSIDE * PPL)


def solution(mesh):
    in_specs = (P(None, ("grp", "dev")), P(("grp", "dev")), P(("grp", "dev")))
    out_specs = P(None, ("grp", "dev"))
    return jax.shard_map(
        on_device, mesh=mesh, in_specs=in_specs, out_specs=out_specs, check_vma=False
    )
```

time: 75.3 us -> 59.3 us (0.79)
  Pallas kernels: 70.8 us -> 57.5 us
  local copies, waits for them, and re-layouts: 4.2 us -> 1.67 us
    pallas_call x3 -> x1, Pallas kernels: 70.8 us -> 57.5 us  [on_device(): pl.pallas_call(functools.partial(whole_kernel, dev_count, bits), out_shap...]
    unnamed x22 -> x1, local copies, waits for them, and re-layouts: 3.25 us -> 1.67 us
    reshape x1 -> x0, local copies, waits for them, and re-layouts: 0.76 us -> none  [on_device(): count = jnp.broadcast_to(leaf_counts.astype(F32).reshape(128, 2, 1), (128...]
where the time goes in v2:
time: 59.3 us; the launch traced here: 59.2 us
  Pallas kernels  57.5 us (97%)
  local copies, waits for them, and re-layouts  1.67 us (3%)
    pallas_call x1, Pallas kernels, on_device(): pl.pallas_call(functools.partial(whole_kernel, dev_count, bits), out_shap...  57.5 us
    unnamed x1, local copies, waits for them, and re-layouts  1.67 us

profile of v2, /device:TPU:1, one launch (start us, length us, event | category | flops | bytes accessed | tf_op | source)
XLA Modules:
  0.0 59.2 jit_solution(9287867907518992156)
XLA Ops:
  0.0 57.5 %fields.1 = f32[512,128]{1,0:T(8,128)} custom-call(f32[256,128]{1,0:T(8,128)} %bitcast.13, f32[128,128]{1,0:T(8,128)} %bitcast.14, s32[2,128]{1,0:T(2,128)} %bitcast.15, s32[16,256]{1,0:T(8,128)} %constant.18.clone.refs_3_, bf16[128,256]{1,0:T(8,128)(2,1)} %constant.19.clone.refs_4_, bf16[128,128]{1,0:T(8,128)(2,1)} %constant.20.clone.refs_5_, ...), custom_call_target="tpu_custom_call" | custom-call | tf_op jit(solution)/shard_map/fields/pallas_call | solution.py:639
  57.5 1.7 %copy.16 = f32[4,16384]{1,0:T(4,128)} copy(f32[4,16384]{1,0:T(4,128)} %bitcast.12) | data formatting | bytes 524288

commit v3 on v2

--- a/solution.py
+++ b/solution.py
@@ -24,6 +24,7 @@
 LANES_OUT = 512
 OFFS = tuple((ox, oy) for ox in (-1, 0, 1) for oy in (-1, 0, 1) if (ox, oy) != (0, 0)) + ((0, 0),)
 NEIGHBOURS = 8
+FILL_LANES = 256
 
 
 def gp_col(gx, gy):
@@ -395,53 +396,56 @@
         def fill(i, carry):
             at = pl.multiple_of(i * 16, 16)
             rows = t_rows[pl.ds(at, 16), :]
-            dx = (rows[:, 0:1] - t_cols[0:1, :]) * scale
-            dy = (rows[:, 1:2] - t_cols[1:2, :]) * scale
-            gap = jnp.maximum(
-                jnp.abs(rows[:, 2:3] - t_cols[2:3, :]), jnp.abs(rows[:, 3:4] - t_cols[3:4, :])
-            )
-            x2 = dx * dx
-            y2 = dy * dy
-            inv = jnp.where(gap > 1.5, 1.0 / (x2 + y2 + SOFTEN), 0.0)
-            inv_sq = inv * inv
-            for c, val in enumerate(
-                (dx * inv, dy * inv, (y2 - x2) * inv_sq, -2.0 * dx * dy * inv_sq)
-            ):
-                hi, lo = split2(val)
-                table_hi[pl.ds(c * 160 + at, 16), :] = hi
-                table_lo[pl.ds(c * 160 + at, 16), :] = lo
+            row_x, row_y = rows[:, 0:1] * scale, rows[:, 1:2] * scale
+            cell_x, cell_y = rows[:, 2:3], rows[:, 3:4]
+            for start in range(0, 1440, FILL_LANES):
+                lanes = slice(start, min(start + FILL_LANES, 1440))
+                dx = row_x - t_cols[0:1, lanes] * scale
+                dy = row_y - t_cols[1:2, lanes] * scale
+                gap = jnp.maximum(
+                    jnp.abs(cell_x - t_cols[2:3, lanes]), jnp.abs(cell_y - t_cols[3:4, lanes])
+                )
+                x2 = dx * dx
+                y2 = dy * dy
+                inv = jnp.where(gap > 1.5, 1.0 / (x2 + y2 + SOFTEN), 0.0)
+                kx = dx * inv
+                ky = dy * inv
+                for c, val in enumerate((kx, ky, ky * ky - kx * kx, -2.0 * kx * ky)):
+                    hi, lo = split2(val)
+                    table_hi[pl.ds(c * 160 + at, 16), lanes] = hi
+                    table_lo[pl.ds(c * 160 + at, 16), lanes] = lo
             return carry
 
         lax.fori_loop(0, 10, fill, 0)
 
     fill_tables(2.0, hi_par, lo_par)
-    mid[...] = lax.fori_loop(1, low_n, add_low, part[...])
-    lax.fori_loop(1, high_n, start_high, 0)
     fill_tables(1.0, hi_leaf, lo_leaf)
 
     def at_offset(o):
-        return pl.ds(pl.multiple_of(o * PPL, PPL), PPL)
-
-    own_rows = jnp.concatenate(own_cut, axis=0)
-
-    def shift_own(o, carry):
-        hot = jnp.where(row256 == src_leaf[pl.ds(o, 1), :], 1.0, 0.0).astype(BF16)
-        moved = tn_none(own_rows, hot)
-        moved = moved[0:192] + moved[192:384] + moved[384:576]
+        return slice(o * PPL, o * PPL + PPL)
+
+    own_parts = jnp.concatenate(own_cut, axis=1)
+
+    def shift_own(o):
+        hot = jnp.where(row256 == src_leaf[o : o + 1, :], 1.0, 0.0).astype(BF16)
+        moved = tn_none(own_parts, jnp.concatenate([hot] * 3, axis=0))
         for tile in (0, 1):
             lanes = slice(tile * 128, tile * 128 + 128)
             su[tile, at_offset(o), :] = moved[0:64, lanes]
             sv[tile, at_offset(o), :] = moved[64:128, lanes]
             sw[tile, at_offset(o), :] = moved[128:192, lanes]
-        return carry
-
-    lax.fori_loop(0, NEIGHBOURS, shift_own, 0)
+
+    for o in range(NEIGHBOURS):
+        shift_own(o)
     self_at = NEIGHBOURS * PPL
     for tile in (0, 1):
         lanes = slice(tile * 128, tile * 128 + 128)
         su[tile, self_at : self_at + PPL, :] = own[0:64, lanes] * 0.5
         sv[tile, self_at : self_at + PPL, :] = own[64:128, lanes] * 0.5
         sw[tile, self_at : self_at + PPL, :] = own[128:192, lanes]
+
+    mid[...] = lax.fori_loop(1, low_n, add_low, part[...])
+    lax.fori_loop(1, high_n, start_high, 0)
 
     zero = jnp.zeros((8, 128), F32)
 
@@ -502,16 +506,13 @@
         (cell_x >= 0.0) & (cell_x < float(nx)) & (cell_y >= 0.0) & (cell_y < float(ny)), 1.0, 0.0
     )
     halo = recv[...].T * inside
-    halo_rows = jnp.concatenate(split3(halo[0:192]), axis=0)
+    halo_parts = jnp.concatenate(split3(halo[0:192]), axis=1)
     row128 = lax.broadcasted_iota(jnp.int32, (128, 256), 0) + 256
 
-    def shift_halo(o, carry):
-        hot = jnp.where(row128 == src_leaf[pl.ds(o, 1), :], 1.0, 0.0).astype(BF16)
-        moved = tn_none(halo_rows, hot)
-        moved = moved[0:192] + moved[192:384] + moved[384:576]
-        skip = o + (o >= 4).astype(jnp.int32)
-        off_x = (skip // 3 - 1).astype(F32)
-        off_y = (skip % 3 - 1).astype(F32)
+    def shift_halo(o):
+        hot = jnp.where(row128 == src_leaf[o : o + 1, :], 1.0, 0.0).astype(BF16)
+        moved = tn_none(halo_parts, jnp.concatenate([hot] * 3, axis=0))
+        off_x, off_y = OFFS[o]
         for tile in (0, 1):
             lanes = slice(tile * 128, tile * 128 + 128)
             at = at_offset(o)
@@ -519,23 +520,22 @@
             sv[tile, at, :] = (sv[tile, at, :] + moved[64:128, lanes]) * 0.5 + off_y
             m = sw[tile, at, :] + moved[128:192, lanes]
             sw[tile, at, :] = jnp.where(m > 0.0, m - mean, 0.0)
-        return carry
-
-    lax.fori_loop(0, NEIGHBOURS, shift_halo, 0)
+
+    for o in range(NEIGHBOURS):
+        shift_halo(o)
 
     all_mom = jnp.concatenate([mom[...], halo[192:512]], axis=1)
     all_mom = all_mom[0:160] - mean * all_mom[160:320]
     cut_mom = jnp.concatenate(split2(all_mom), axis=0)
 
-    def shift_moments(o, carry):
-        hot = jnp.where(row256[:, 0:128] == src_mom[pl.ds(o, 1), :], 1.0, 0.0).astype(BF16)
+    def shift_moments(o):
+        hot = jnp.where(row256[:, 0:128] == src_mom[o : o + 1, :], 1.0, 0.0).astype(BF16)
         moved = tn_none(cut_mom, hot).astype(BF16)
-        at = pl.ds(pl.multiple_of(o * 160, 32), 160)
-        xs[at, 0:128] = moved[0:160]
-        xs[at, 128:256] = moved[160:320]
-        return carry
-
-    lax.fori_loop(0, 9, shift_moments, 0)
+        xs[o * 160 : o * 160 + 160, 0:128] = moved[0:160]
+        xs[o * 160 : o * 160 + 160, 128:256] = moved[160:320]
+
+    for o in range(9):
+        shift_moments(o)
 
     def far(table_hi, table_lo):
         wide = tn_none(table_hi[...], xs[...])

time: 59.3 us -> 53.7 us (0.906)
  Pallas kernels: 57.5 us -> 51.9 us
    pallas_call x1, Pallas kernels: 57.5 us -> 51.9 us  [on_device(): pl.pallas_call(functools.partial(whole_kernel, dev_count, bits), out_shap...]
where the time goes in v3:
time: 53.7 us; the launch traced here: 53.6 us
  Pallas kernels  51.9 us (97%)
  local copies, waits for them, and re-layouts  1.67 us (3%)
    pallas_call x1, Pallas kernels, on_device(): pl.pallas_call(functools.partial(whole_kernel, dev_count, bits), out_shap...  51.9 us
    unnamed x1, local copies, waits for them, and re-layouts  1.67 us

profile of v3, /device:TPU:1, one launch (start us, length us, event | category | flops | bytes accessed | tf_op | source)
XLA Modules:
  0.0 53.6 jit_solution(14547174280391770936)
XLA Ops:
  0.0 51.9 %fields.1 = f32[512,128]{1,0:T(8,128)} custom-call(f32[256,128]{1,0:T(8,128)} %bitcast.13, f32[128,128]{1,0:T(8,128)} %bitcast.14, s32[2,128]{1,0:T(2,128)} %bitcast.15, s32[16,256]{1,0:T(8,128)} %constant.18.clone.refs_3_, bf16[128,256]{1,0:T(8,128)(2,1)} %constant.19.clone.refs_4_, bf16[128,128]{1,0:T(8,128)(2,1)} %constant.20.clone.refs_5_, ...), custom_call_target="tpu_custom_call" | custom-call | tf_op jit(solution)/shard_map/fields/pallas_call | solution.py:639
  51.9 1.7 %copy.16 = f32[4,16384]{1,0:T(4,128)} copy(f32[4,16384]{1,0:T(4,128)} %bitcast.12) | data formatting | bytes 524288

commit v4 on v3

--- a/solution.py
+++ b/solution.py
@@ -232,7 +232,7 @@
 
 def run_kernel(dev_count, bits, arrivals, pos, mass, count, sel_leaf, sel_mom, up, down, sides,
                src_leaf, src_mom, t_rows, t_cols, out, own, mom, send, recv, part, mid, leaf_mom, first,
-                 second, su, sv, sw, lone, xs, hi_leaf, lo_leaf, hi_par, lo_par, leaf_local,
+                 second, su, sv, sw, lone, xs, xs_par, hi_leaf, lo_leaf, hi_par, lo_par, leaf_kind, leaf_local,
                  result, self_live, edge_s, edge_r, sum_s1, sum_r1, sum_s2, sum_r2):
     code = lax.axis_index("grp") * dev_count + lax.axis_index("dev")
     bx, by = morton_split(code, bits)
@@ -300,10 +300,6 @@
         totals[0] + totals[1],
         jnp.where(row == 1, counts[:, 0:128] + counts[:, 128:256], 0.0),
     )
-    for k in (0, 1):
-        vals = turned(pos, k, 2)
-        own[k * PPL : (k + 1) * PPL, 0:128] = vals[:PPL]
-        own[k * PPL : (k + 1) * PPL, 128:256] = vals[PPL:]
 
     def low_copy(k):
         return pltpu.make_async_remote_copy(
@@ -335,6 +331,10 @@
 
     pl.semaphore_wait(barrier, 8 + low_n - 1 + high_n - 1)
     lax.fori_loop(1, low_n, start_low, 0)
+    for k in (0, 1):
+        vals = turned(pos, k, 2)
+        own[k * PPL : (k + 1) * PPL, 0:128] = vals[:PPL]
+        own[k * PPL : (k + 1) * PPL, 128:256] = vals[PPL:]
 
     for arrival in arrivals[4:]:
         arrival.wait()
@@ -494,10 +494,6 @@
                     result[c, rows, :] = acc[8 * t + c] * scale
                     self_live[c, rows, :] = acc[8 * t + 4 + c] * scale
 
-    sums = lax.fori_loop(1, high_n, add_high, mid[...])
-    mass_sum = jnp.sum(sums[0:1], axis=1, keepdims=True)
-    live_sum = jnp.sum(sums[1:2], axis=1, keepdims=True)
-    mean = mass_sum / live_sum
     for copy in edges:
         copy.wait()
     cell_x = sides[0:1] + jnp.full((1, 128), bx, jnp.int32).astype(F32)
@@ -518,52 +514,62 @@
             at = at_offset(o)
             su[tile, at, :] = (su[tile, at, :] + moved[0:64, lanes]) * 0.5 + off_x
             sv[tile, at, :] = (sv[tile, at, :] + moved[64:128, lanes]) * 0.5 + off_y
-            m = sw[tile, at, :] + moved[128:192, lanes]
-            sw[tile, at, :] = jnp.where(m > 0.0, m - mean, 0.0)
+            sw[tile, at, :] = sw[tile, at, :] + moved[128:192, lanes]
 
     for o in range(NEIGHBOURS):
         shift_halo(o)
 
     all_mom = jnp.concatenate([mom[...], halo[192:512]], axis=1)
-    all_mom = all_mom[0:160] - mean * all_mom[160:320]
     cut_mom = jnp.concatenate(split2(all_mom), axis=0)
 
     def shift_moments(o):
         hot = jnp.where(row256[:, 0:128] == src_mom[o : o + 1, :], 1.0, 0.0).astype(BF16)
-        moved = tn_none(cut_mom, hot).astype(BF16)
-        xs[o * 160 : o * 160 + 160, 0:128] = moved[0:160]
-        xs[o * 160 : o * 160 + 160, 128:256] = moved[160:320]
+        moved = tn_none(cut_mom, hot)
+        at = slice(o * 160, o * 160 + 160)
+        pieces = [moved[160 * i : 160 * i + 160] for i in range(4)]
+        xs[at, :] = jnp.concatenate([p[:, 0:64] for p in pieces], axis=1).astype(BF16)
+        xs_par[at, :] = jnp.concatenate([p[:, 64:80] for p in pieces], axis=1).astype(BF16)
 
     for o in range(9):
         shift_moments(o)
 
-    def far(table_hi, table_lo):
-        wide = tn_none(table_hi[...], xs[...])
-        return wide[:, 0:128] + wide[:, 128:256] + tn_none(table_lo[...], xs[:, 0:128])
-
-    par = far(hi_par, lo_par)
+    wide = tn_none(hi_par[...], xs_par[...])
+    par = wide[:, 0:32] + wide[:, 32:64] + tn_none(lo_par[...], xs_par[:, 0:32])
     par_cols = jnp.concatenate(
         [
-            jnp.concatenate(
-                [par[c * 160 + q * NM : c * 160 + q * NM + NM, 64:80] for q in range(4)], axis=1
-            )
+            par[c * 160 + q * NM : c * 160 + q * NM + NM, kind * 16 : kind * 16 + 16]
+            for kind in (0, 1)
             for c in range(4)
+            for q in range(4)
         ],
         axis=1,
     )
     from_par = jnp.dot(
         down[...], par_cols, precision=HIGHEST, preferred_element_type=F32
     )
-    leaf = far(hi_leaf, lo_leaf)
+    wide = tn_none(hi_leaf[...], xs[...])
+    leaf = wide[:, 0:128] + wide[:, 128:256] + tn_none(lo_leaf[...], xs[:, 0:128])
+    for kind in (0, 1):
+        for c in range(4):
+            at = kind * 256 + c * 64
+            leaf_kind[kind, c] = jnp.concatenate(
+                [
+                    leaf[c * 160 + ch * NM : c * 160 + ch * NM + NM, kind * 64 : kind * 64 + 64]
+                    + from_par[ch * NM : ch * NM + NM, at : at + 64]
+                    for ch in range(4)
+                ],
+                axis=1,
+            )
+
+    sums = lax.fori_loop(1, high_n, add_high, mid[...])
+    mass_sum = jnp.sum(sums[0:1], axis=1, keepdims=True)
+    live_sum = jnp.sum(sums[1:2], axis=1, keepdims=True)
+    mean = mass_sum / live_sum
+    for tile in (0, 1):
+        m = sw[tile, 0:self_at, :]
+        sw[tile, 0:self_at, :] = jnp.where(m > 0.0, m - mean, 0.0)
     for c in range(4):
-        leaf_local[c] = jnp.concatenate(
-            [
-                leaf[c * 160 + ch * NM : c * 160 + ch * NM + NM, 0:64]
-                + from_par[ch * NM : ch * NM + NM, c * 64 : c * 64 + 64]
-                for ch in range(4)
-            ],
-            axis=1,
-        )
+        leaf_local[c] = leaf_kind[0, c] - mean * leaf_kind[1, c]
 
     for tile in (0, 1):
         lanes = slice(tile * 128, tile * 128 + 128)
@@ -579,7 +585,7 @@
                 acc = acc + half * bu[a]
             result[c, rows, :] = acc
 
-    width, unroll = 4, 8
+    width, unroll = 4, 16
     for tile in (0, 1):
         for piece in range(PPL // (8 * width)):
             base = piece * 8 * width
@@ -593,15 +599,15 @@
                     for t in range(width):
                         dx = tx[t] - sx
                         dy = ty[t] - sy
-                        x2 = dx * dx
-                        y2 = dy * dy
-                        inv = 1.0 / (x2 + y2 + SOFTEN)
-                        w1 = w * inv
-                        w2 = w1 * inv
-                        acc[4 * t] = acc[4 * t] + w1 * dx
-                        acc[4 * t + 1] = acc[4 * t + 1] + w1 * dy
-                        acc[4 * t + 2] = acc[4 * t + 2] + w2 * (y2 - x2)
-                        acc[4 * t + 3] = acc[4 * t + 3] + w2 * (dx * dy)
+                        inv = 1.0 / (dy * dy + (dx * dx + SOFTEN))
+                        kx = dx * inv
+                        ky = dy * inv
+                        wx = w * kx
+                        wy = w * ky
+                        acc[4 * t] = acc[4 * t] + wx
+                        acc[4 * t + 1] = acc[4 * t + 1] + wy
+                        acc[4 * t + 2] = (acc[4 * t + 2] + wy * ky) - wx * kx
+                        acc[4 * t + 3] = acc[4 * t + 3] + wx * ky
                 return tuple(acc)
 
             acc = lax.fori_loop(0, NEIGHBOURS * PPL // unroll, pairs, (zero,) * (4 * width))
@@ -658,10 +664,12 @@
             pltpu.VMEM((2, 9 * PPL + 8, 128), F32),
             pltpu.VMEM((2, PPL + 8, 128), F32),
             pltpu.VMEM((1440, 256), BF16),
+            pltpu.VMEM((1440, 64), BF16),
             pltpu.VMEM((640, 1440), BF16),
             pltpu.VMEM((640, 1440), BF16),
             pltpu.VMEM((640, 1440), BF16),
             pltpu.VMEM((640, 1440), BF16),
+            pltpu.VMEM((2, 4, NM, 256), F32),
             pltpu.VMEM((4, NM, 256), F32),
             pltpu.VMEM((4, 128, 128), F32),
             pltpu.VMEM((4, 128, 128), F32),

time: 53.7 us -> 53.6 us (level)
  no operation moved by 1% of the time
where the time goes in v4:
time: 53.6 us; the launch traced here: 53.5 us
  Pallas kernels  51.8 us (97%)
  local copies, waits for them, and re-layouts  1.67 us (3%)
    pallas_call x1, Pallas kernels, on_device(): pl.pallas_call(functools.partial(whole_kernel, dev_count, bits), out_shap...  51.8 us
    unnamed x1, local copies, waits for them, and re-layouts  1.67 us

profile of v4, /device:TPU:1, one launch (start us, length us, event | category | flops | bytes accessed | tf_op | source)
XLA Modules:
  0.0 53.5 jit_solution(5788237754581126506)
XLA Ops:
  0.0 51.8 %fields.1 = f32[512,128]{1,0:T(8,128)} custom-call(f32[256,128]{1,0:T(8,128)} %bitcast.13, f32[128,128]{1,0:T(8,128)} %bitcast.14, s32[2,128]{1,0:T(2,128)} %bitcast.15, s32[16,256]{1,0:T(8,128)} %constant.18.clone.refs_3_, bf16[128,256]{1,0:T(8,128)(2,1)} %constant.19.clone.refs_4_, bf16[128,128]{1,0:T(8,128)(2,1)} %constant.20.clone.refs_5_, ...), custom_call_target="tpu_custom_call" | custom-call | tf_op jit(solution)/shard_map/fields/pallas_call | solution.py:645
  51.8 1.7 %copy.16 = f32[4,16384]{1,0:T(4,128)} copy(f32[4,16384]{1,0:T(4,128)} %bitcast.12) | data formatting | bytes 524288

commit v5 on v3

--- a/solution.py
+++ b/solution.py
@@ -232,8 +232,8 @@
 
 def run_kernel(dev_count, bits, arrivals, pos, mass, count, sel_leaf, sel_mom, up, down, sides,
                src_leaf, src_mom, t_rows, t_cols, out, own, mom, send, recv, part, mid, leaf_mom, first,
-                 second, su, sv, sw, lone, xs, hi_leaf, lo_leaf, hi_par, lo_par, leaf_local,
-                 result, self_live, edge_s, edge_r, sum_s1, sum_r1, sum_s2, sum_r2):
+                 second, su, sv, sw, xs, hi_leaf, lo_leaf, hi_par, lo_par, leaf_local,
+                 result, edge_s, edge_r, sum_s1, sum_r1, sum_s2, sum_r2):
     code = lax.axis_index("grp") * dev_count + lax.axis_index("dev")
     bx, by = morton_split(code, bits)
     nx, ny = 2 ** ((bits + 1) // 2), 2 ** (bits // 2)
@@ -300,10 +300,6 @@
         totals[0] + totals[1],
         jnp.where(row == 1, counts[:, 0:128] + counts[:, 128:256], 0.0),
     )
-    for k in (0, 1):
-        vals = turned(pos, k, 2)
-        own[k * PPL : (k + 1) * PPL, 0:128] = vals[:PPL]
-        own[k * PPL : (k + 1) * PPL, 128:256] = vals[PPL:]
 
     def low_copy(k):
         return pltpu.make_async_remote_copy(
@@ -335,6 +331,10 @@
 
     pl.semaphore_wait(barrier, 8 + low_n - 1 + high_n - 1)
     lax.fori_loop(1, low_n, start_low, 0)
+    for k in (0, 1):
+        vals = turned(pos, k, 2)
+        own[k * PPL : (k + 1) * PPL, 0:128] = vals[:PPL]
+        own[k * PPL : (k + 1) * PPL, 128:256] = vals[PPL:]
 
     for arrival in arrivals[4:]:
         arrival.wait()
@@ -345,7 +345,6 @@
         bv = basis(own[64:128, lanes])
         m_t = own[128:192, lanes]
         live_t = jnp.where(m_t > 0.0, 1.0, 0.0)
-        lone[tile, 0:PPL, :] = live_t
         for kind, weight in enumerate((m_t, live_t)):
             for a in range(NODES):
                 wa = bu[a] * weight
@@ -391,6 +390,8 @@
         copy.start()
         edges.append(copy)
     recv[96:HROWS, :] = jnp.zeros((HROWS - 96, LANES_OUT), F32)
+    mid[...] = lax.fori_loop(1, low_n, add_low, part[...])
+    lax.fori_loop(1, high_n, start_high, 0)
 
     def fill_tables(scale, table_hi, table_lo):
         def fill(i, carry):
@@ -437,17 +438,17 @@
 
     for o in range(NEIGHBOURS):
         shift_own(o)
+    sums = lax.fori_loop(1, high_n, add_high, mid[...])
+    mass_sum = jnp.sum(sums[0:1], axis=1, keepdims=True)
+    live_sum = jnp.sum(sums[1:2], axis=1, keepdims=True)
+    mean = mass_sum / live_sum
     self_at = NEIGHBOURS * PPL
     for tile in (0, 1):
         lanes = slice(tile * 128, tile * 128 + 128)
         su[tile, self_at : self_at + PPL, :] = own[0:64, lanes] * 0.5
         sv[tile, self_at : self_at + PPL, :] = own[64:128, lanes] * 0.5
-        sw[tile, self_at : self_at + PPL, :] = own[128:192, lanes]
-
-    mid[...] = lax.fori_loop(1, low_n, add_low, part[...])
-    lax.fori_loop(1, high_n, start_high, 0)
-
-    zero = jnp.zeros((8, 128), F32)
+        m = own[128:192, lanes]
+        sw[tile, self_at : self_at + PPL, :] = jnp.where(m > 0.0, m - mean, 0.0)
 
     def targets(tile, base, width):
         lanes = slice(tile * 128, tile * 128 + 128)
@@ -455,49 +456,44 @@
         ty = [own[64 + base + 8 * i : 72 + base + 8 * i, lanes] * 0.5 for i in range(width)]
         return tx, ty
 
-    self_width = 2
-    for tile in (0, 1):
-        for piece in range(PPL // (8 * self_width)):
-            base = piece * 8 * self_width
-            tx, ty = targets(tile, base, self_width)
-
-            def self_pairs(step, acc, tile=tile, tx=tx, ty=ty):
-                acc = list(acc)
-                for i in range(4):
-                    k = step * 4 + i
-                    at = pl.ds(self_at + k, 8, stride=0)
-                    sx, sy, m = su[tile, at, :], sv[tile, at, :], sw[tile, at, :]
-                    one = lone[tile, pl.ds(k, 8, stride=0), :]
-                    for t in range(self_width):
-                        dx = tx[t] - sx
-                        dy = ty[t] - sy
-                        x2 = dx * dx
-                        y2 = dy * dy
-                        inv = 1.0 / (x2 + y2 + SOFTEN)
-                        gap = y2 - x2
-                        cross = dx * dy
-                        for kind, w in enumerate((m, one)):
-                            at_acc = 8 * t + 4 * kind
-                            w1 = w * inv
-                            w2 = w1 * inv
-                            acc[at_acc] = acc[at_acc] + w1 * dx
-                            acc[at_acc + 1] = acc[at_acc + 1] + w1 * dy
-                            acc[at_acc + 2] = acc[at_acc + 2] + w2 * gap
-                            acc[at_acc + 3] = acc[at_acc + 3] + w2 * cross
-                return tuple(acc)
-
-            acc = lax.fori_loop(0, PPL // 4, self_pairs, (zero,) * (8 * self_width))
-            for t in range(self_width):
-                rows = slice(tile * PPL + base + 8 * t, tile * PPL + base + 8 * t + 8)
-                for c in range(4):
-                    scale = -2.0 if c == 3 else 1.0
-                    result[c, rows, :] = acc[8 * t + c] * scale
-                    self_live[c, rows, :] = acc[8 * t + 4 + c] * scale
-
-    sums = lax.fori_loop(1, high_n, add_high, mid[...])
-    mass_sum = jnp.sum(sums[0:1], axis=1, keepdims=True)
-    live_sum = jnp.sum(sums[1:2], axis=1, keepdims=True)
-    mean = mass_sum / live_sum
+    def near_field(first_row, row_count, fresh):
+        width, unroll = 4, 16
+        zero = jnp.zeros((8, 128), F32)
+        for tile in (0, 1):
+            for piece in range(PPL // (8 * width)):
+                base = piece * 8 * width
+                tx, ty = targets(tile, base, width)
+
+                def pairs(step, acc, tile=tile, tx=tx, ty=ty):
+                    acc = list(acc)
+                    for i in range(unroll):
+                        at = pl.ds(first_row + step * unroll + i, 8, stride=0)
+                        sx, sy, w = su[tile, at, :], sv[tile, at, :], sw[tile, at, :]
+                        for t in range(width):
+                            dx = tx[t] - sx
+                            dy = ty[t] - sy
+                            inv = 1.0 / (dy * dy + (dx * dx + SOFTEN))
+                            kx = dx * inv
+                            ky = dy * inv
+                            wx = w * kx
+                            wy = w * ky
+                            acc[4 * t] = acc[4 * t] + wx
+                            acc[4 * t + 1] = acc[4 * t + 1] + wy
+                            acc[4 * t + 2] = (acc[4 * t + 2] + wy * ky) - wx * kx
+                            acc[4 * t + 3] = acc[4 * t + 3] + wx * ky
+                    return tuple(acc)
+
+                acc = lax.fori_loop(0, row_count // unroll, pairs, (zero,) * (4 * width))
+                for t in range(width):
+                    rows = slice(tile * PPL + base + 8 * t, tile * PPL + base + 8 * t + 8)
+                    for c in range(4):
+                        near = acc[4 * t + c]
+                        if c == 3:
+                            near = near * -2.0
+                        result[c, rows, :] = near if fresh else result[c, rows, :] + near
+
+    near_field(self_at, PPL, True)
+
     for copy in edges:
         copy.wait()
     cell_x = sides[0:1] + jnp.full((1, 128), bx, jnp.int32).astype(F32)
@@ -571,7 +567,7 @@
         bv = basis(own[64:128, lanes])
         for c in range(4):
             rows = slice(tile * PPL, tile * PPL + PPL)
-            acc = result[c, rows, :] - mean * self_live[c, rows, :]
+            acc = result[c, rows, :]
             for a in range(NODES):
                 half = leaf_local[c, pl.ds(a * 6, 1), lanes] * bv[0]
                 for b in range(1, NODES):
@@ -579,39 +575,7 @@
                 acc = acc + half * bu[a]
             result[c, rows, :] = acc
 
-    width, unroll = 4, 8
-    for tile in (0, 1):
-        for piece in range(PPL // (8 * width)):
-            base = piece * 8 * width
-            tx, ty = targets(tile, base, width)
-
-            def pairs(step, acc, tile=tile, tx=tx, ty=ty):
-                acc = list(acc)
-                for i in range(unroll):
-                    at = pl.ds(step * unroll + i, 8, stride=0)
-                    sx, sy, w = su[tile, at, :], sv[tile, at, :], sw[tile, at, :]
-                    for t in range(width):
-                        dx = tx[t] - sx
-                        dy = ty[t] - sy
-                        x2 = dx * dx
-                        y2 = dy * dy
-                        inv = 1.0 / (x2 + y2 + SOFTEN)
-                        w1 = w * inv
-                        w2 = w1 * inv
-                        acc[4 * t] = acc[4 * t] + w1 * dx
-                        acc[4 * t + 1] = acc[4 * t + 1] + w1 * dy
-                        acc[4 * t + 2] = acc[4 * t + 2] + w2 * (y2 - x2)
-                        acc[4 * t + 3] = acc[4 * t + 3] + w2 * (dx * dy)
-                return tuple(acc)
-
-            acc = lax.fori_loop(0, NEIGHBOURS * PPL // unroll, pairs, (zero,) * (4 * width))
-            for t in range(width):
-                rows = slice(tile * PPL + base + 8 * t, tile * PPL + base + 8 * t + 8)
-                for c in range(4):
-                    near = acc[4 * t + c]
-                    if c == 3:
-                        near = near * -2.0
-                    result[c, rows, :] = result[c, rows, :] + near
+    near_field(0, self_at, False)
 
     for c in range(4):
         back = result[c].T
@@ -656,14 +620,12 @@
             pltpu.VMEM((2, 9 * PPL + 8, 128), F32),
             pltpu.VMEM((2, 9 * PPL + 8, 128), F32),
             pltpu.VMEM((2, 9 * PPL + 8, 128), F32),
-            pltpu.VMEM((2, PPL + 8, 128), F32),
             pltpu.VMEM((1440, 256), BF16),
             pltpu.VMEM((640, 1440), BF16),
             pltpu.VMEM((640, 1440), BF16),
             pltpu.VMEM((640, 1440), BF16),
             pltpu.VMEM((640, 1440), BF16),
             pltpu.VMEM((4, NM, 256), F32),
-            pltpu.VMEM((4, 128, 128), F32),
             pltpu.VMEM((4, 128, 128), F32),
             pltpu.SemaphoreType.DMA((8,)),
             pltpu.SemaphoreType.DMA((8,)),

time: 53.7 us -> 54 us (level)
  no operation moved by 1% of the time
where the time goes in v5:
time: 54 us; the launch traced here: 53.8 us
  Pallas kernels  52.2 us (97%)
  local copies, waits for them, and re-layouts  1.67 us (3%)
    pallas_call x1, Pallas kernels, on_device(): pl.pallas_call(functools.partial(whole_kernel, dev_count, bits), out_shap...  52.2 us
    unnamed x1, local copies, waits for them, and re-layouts  1.67 us

profile of v5, /device:TPU:1, one launch (start us, length us, event | category | flops | bytes accessed | tf_op | source)
XLA Modules:
  0.0 53.8 jit_solution(2964714302212666372)
XLA Ops:
  0.0 52.2 %fields.1 = f32[512,128]{1,0:T(8,128)} custom-call(f32[256,128]{1,0:T(8,128)} %bitcast.13, f32[128,128]{1,0:T(8,128)} %bitcast.14, s32[2,128]{1,0:T(2,128)} %bitcast.15, s32[16,256]{1,0:T(8,128)} %constant.18.clone.refs_3_, bf16[128,256]{1,0:T(8,128)(2,1)} %constant.19.clone.refs_4_, bf16[128,128]{1,0:T(8,128)(2,1)} %constant.20.clone.refs_5_, ...), custom_call_target="tpu_custom_call" | custom-call | tf_op jit(solution)/shard_map/fields/pallas_call | solution.py:603
  52.2 1.7 %copy.16 = f32[4,16384]{1,0:T(4,128)} copy(f32[4,16384]{1,0:T(4,128)} %bitcast.12) | data formatting | bytes 524288

commit v6 on v5

--- a/solution.py
+++ b/solution.py
@@ -224,15 +224,15 @@
         pltpu.make_async_copy(src, dst, arrive_sems.at[i])
         for i, (src, dst) in enumerate(zip(sources, held))
     ]
-    for arrival in arrivals:
-        arrival.start()
+    for i in (1, 2, 3, 0, *range(4, OPERANDS)):
+        arrivals[i].start()
     run_kernel(dev_count, bits, arrivals, pos, mass, count, sel_leaf, sel_mom, up, down, sides,
                src_leaf, src_mom, t_rows, t_cols, out, *refs[1:])
 
 
 def run_kernel(dev_count, bits, arrivals, pos, mass, count, sel_leaf, sel_mom, up, down, sides,
                src_leaf, src_mom, t_rows, t_cols, out, own, mom, send, recv, part, mid, leaf_mom, first,
-                 second, su, sv, sw, xs, hi_leaf, lo_leaf, hi_par, lo_par, leaf_local,
+                 second, su, sv, sw, xs, xs_par, hi_leaf, lo_leaf, hi_par, lo_par, leaf_kind, leaf_local,
                  result, edge_s, edge_r, sum_s1, sum_r1, sum_s2, sum_r2):
     code = lax.axis_index("grp") * dev_count + lax.axis_index("dev")
     bx, by = morton_split(code, bits)
@@ -279,7 +279,7 @@
         )
         return rows.T
 
-    for arrival in arrivals[:4]:
+    for arrival in arrivals[1:4]:
         arrival.wait()
     row256 = lax.broadcasted_iota(jnp.int32, (256, 256), 0)
     pick = jnp.where(row256 == src_leaf[9:10, :], 1.0, 0.0).astype(BF16)
@@ -294,6 +294,9 @@
         vals = jnp.where(live, m_turned[tile * PPL : tile * PPL + PPL], 0.0)
         own[128:192, lanes] = vals
         totals.append(jnp.sum(vals, axis=0, keepdims=True))
+    near_mean = jnp.sum(totals[0] + totals[1], axis=1, keepdims=True) / jnp.sum(
+        counts, axis=1, keepdims=True
+    )
     row = lax.broadcasted_iota(jnp.int32, (8, 128), 0)
     part[...] = jnp.where(
         row == 0,
@@ -331,6 +334,7 @@
 
     pl.semaphore_wait(barrier, 8 + low_n - 1 + high_n - 1)
     lax.fori_loop(1, low_n, start_low, 0)
+    arrivals[0].wait()
     for k in (0, 1):
         vals = turned(pos, k, 2)
         own[k * PPL : (k + 1) * PPL, 0:128] = vals[:PPL]
@@ -438,17 +442,12 @@
 
     for o in range(NEIGHBOURS):
         shift_own(o)
-    sums = lax.fori_loop(1, high_n, add_high, mid[...])
-    mass_sum = jnp.sum(sums[0:1], axis=1, keepdims=True)
-    live_sum = jnp.sum(sums[1:2], axis=1, keepdims=True)
-    mean = mass_sum / live_sum
     self_at = NEIGHBOURS * PPL
     for tile in (0, 1):
         lanes = slice(tile * 128, tile * 128 + 128)
         su[tile, self_at : self_at + PPL, :] = own[0:64, lanes] * 0.5
         sv[tile, self_at : self_at + PPL, :] = own[64:128, lanes] * 0.5
-        m = own[128:192, lanes]
-        sw[tile, self_at : self_at + PPL, :] = jnp.where(m > 0.0, m - mean, 0.0)
+        sw[tile, self_at : self_at + PPL, :] = own[128:192, lanes]
 
     def targets(tile, base, width):
         lanes = slice(tile * 128, tile * 128 + 128)
@@ -456,7 +455,7 @@
         ty = [own[64 + base + 8 * i : 72 + base + 8 * i, lanes] * 0.5 for i in range(width)]
         return tx, ty
 
-    def near_field(first_row, row_count, fresh):
+    def near_field(first_row, row_count):
         width, unroll = 4, 16
         zero = jnp.zeros((8, 128), F32)
         for tile in (0, 1):
@@ -490,9 +489,7 @@
                         near = acc[4 * t + c]
                         if c == 3:
                             near = near * -2.0
-                        result[c, rows, :] = near if fresh else result[c, rows, :] + near
-
-    near_field(self_at, PPL, True)
+                        result[c, rows, :] = result[c, rows, :] + near
 
     for copy in edges:
         copy.wait()
@@ -514,52 +511,65 @@
             at = at_offset(o)
             su[tile, at, :] = (su[tile, at, :] + moved[0:64, lanes]) * 0.5 + off_x
             sv[tile, at, :] = (sv[tile, at, :] + moved[64:128, lanes]) * 0.5 + off_y
-            m = sw[tile, at, :] + moved[128:192, lanes]
-            sw[tile, at, :] = jnp.where(m > 0.0, m - mean, 0.0)
+            sw[tile, at, :] = sw[tile, at, :] + moved[128:192, lanes]
 
     for o in range(NEIGHBOURS):
         shift_halo(o)
 
     all_mom = jnp.concatenate([mom[...], halo[192:512]], axis=1)
-    all_mom = all_mom[0:160] - mean * all_mom[160:320]
+    all_mom = jnp.concatenate(
+        [all_mom[0:160] - near_mean * all_mom[160:320], all_mom[160:320]], axis=0
+    )
     cut_mom = jnp.concatenate(split2(all_mom), axis=0)
 
     def shift_moments(o):
         hot = jnp.where(row256[:, 0:128] == src_mom[o : o + 1, :], 1.0, 0.0).astype(BF16)
-        moved = tn_none(cut_mom, hot).astype(BF16)
-        xs[o * 160 : o * 160 + 160, 0:128] = moved[0:160]
-        xs[o * 160 : o * 160 + 160, 128:256] = moved[160:320]
+        moved = tn_none(cut_mom, hot)
+        at = slice(o * 160, o * 160 + 160)
+        pieces = [moved[160 * i : 160 * i + 160] for i in range(4)]
+        xs[at, :] = jnp.concatenate([p[:, 0:64] for p in pieces], axis=1).astype(BF16)
+        xs_par[at, :] = jnp.concatenate([p[:, 64:80] for p in pieces], axis=1).astype(BF16)
 
     for o in range(9):
         shift_moments(o)
 
-    def far(table_hi, table_lo):
-        wide = tn_none(table_hi[...], xs[...])
-        return wide[:, 0:128] + wide[:, 128:256] + tn_none(table_lo[...], xs[:, 0:128])
-
-    par = far(hi_par, lo_par)
+    wide = tn_none(hi_par[...], xs_par[...])
+    par = wide[:, 0:32] + wide[:, 32:64] + tn_none(lo_par[...], xs_par[:, 0:32])
     par_cols = jnp.concatenate(
         [
-            jnp.concatenate(
-                [par[c * 160 + q * NM : c * 160 + q * NM + NM, 64:80] for q in range(4)], axis=1
-            )
+            par[c * 160 + q * NM : c * 160 + q * NM + NM, kind * 16 : kind * 16 + 16]
+            for kind in (0, 1)
             for c in range(4)
+            for q in range(4)
         ],
         axis=1,
     )
     from_par = jnp.dot(
         down[...], par_cols, precision=HIGHEST, preferred_element_type=F32
     )
-    leaf = far(hi_leaf, lo_leaf)
+    wide = tn_none(hi_leaf[...], xs[...])
+    leaf = wide[:, 0:128] + wide[:, 128:256] + tn_none(lo_leaf[...], xs[:, 0:128])
+    for kind in (0, 1):
+        for c in range(4):
+            at = kind * 256 + c * 64
+            leaf_kind[kind, c] = jnp.concatenate(
+                [
+                    leaf[c * 160 + ch * NM : c * 160 + ch * NM + NM, kind * 64 : kind * 64 + 64]
+                    + from_par[ch * NM : ch * NM + NM, at : at + 64]
+                    for ch in range(4)
+                ],
+                axis=1,
+            )
+
+    sums = lax.fori_loop(1, high_n, add_high, mid[...])
+    mass_sum = jnp.sum(sums[0:1], axis=1, keepdims=True)
+    live_sum = jnp.sum(sums[1:2], axis=1, keepdims=True)
+    mean = mass_sum / live_sum
+    for tile in (0, 1):
+        m = sw[tile, 0 : 9 * PPL, :]
+        sw[tile, 0 : 9 * PPL, :] = jnp.where(m > 0.0, m - mean, 0.0)
     for c in range(4):
-        leaf_local[c] = jnp.concatenate(
-            [
-                leaf[c * 160 + ch * NM : c * 160 + ch * NM + NM, 0:64]
-                + from_par[ch * NM : ch * NM + NM, c * 64 : c * 64 + 64]
-                for ch in range(4)
-            ],
-            axis=1,
-        )
+        leaf_local[c] = leaf_kind[0, c] - (mean - near_mean) * leaf_kind[1, c]
 
     for tile in (0, 1):
         lanes = slice(tile * 128, tile * 128 + 128)
@@ -567,15 +577,15 @@
         bv = basis(own[64:128, lanes])
         for c in range(4):
             rows = slice(tile * PPL, tile * PPL + PPL)
-            acc = result[c, rows, :]
+            acc = None
             for a in range(NODES):
                 half = leaf_local[c, pl.ds(a * 6, 1), lanes] * bv[0]
                 for b in range(1, NODES):
                     half = half + leaf_local[c, pl.ds(a * 6 + b, 1), lanes] * bv[b]
-                acc = acc + half * bu[a]
+                acc = half * bu[a] if acc is None else acc + half * bu[a]
             result[c, rows, :] = acc
 
-    near_field(0, self_at, False)
+    near_field(0, 9 * PPL)
 
     for c in range(4):
         back = result[c].T
@@ -621,10 +631,12 @@
             pltpu.VMEM((2, 9 * PPL + 8, 128), F32),
             pltpu.VMEM((2, 9 * PPL + 8, 128), F32),
             pltpu.VMEM((1440, 256), BF16),
+            pltpu.VMEM((1440, 64), BF16),
             pltpu.VMEM((640, 1440), BF16),
             pltpu.VMEM((640, 1440), BF16),
             pltpu.VMEM((640, 1440), BF16),
             pltpu.VMEM((640, 1440), BF16),
+            pltpu.VMEM((2, 4, NM, 256), F32),
             pltpu.VMEM((4, NM, 256), F32),
             pltpu.VMEM((4, 128, 128), F32),
             pltpu.SemaphoreType.DMA((8,)),

time: 54 us -> 54.6 us (1.011)
  Pallas kernels: 52.2 us -> 52.8 us
    pallas_call x1, Pallas kernels: 52.2 us -> 52.8 us  [on_device(): pl.pallas_call(functools.partial(whole_kernel, dev_count, bits), out_shap...]
where the time goes in v6:
time: 54.6 us; the launch traced here: 54.4 us
  Pallas kernels  52.8 us (97%)
  local copies, waits for them, and re-layouts  1.67 us (3%)
    pallas_call x1, Pallas kernels, on_device(): pl.pallas_call(functools.partial(whole_kernel, dev_count, bits), out_shap...  52.8 us
    unnamed x1, local copies, waits for them, and re-layouts  1.67 us

profile of v6, /device:TPU:1, one launch (start us, length us, event | category | flops | bytes accessed | tf_op | source)
XLA Modules:
  0.0 54.4 jit_solution(12018748777062501133)
XLA Ops:
  0.0 52.8 %fields.1 = f32[512,128]{1,0:T(8,128)} custom-call(f32[256,128]{1,0:T(8,128)} %bitcast.13, f32[128,128]{1,0:T(8,128)} %bitcast.14, s32[2,128]{1,0:T(2,128)} %bitcast.15, s32[16,256]{1,0:T(8,128)} %constant.18.clone.refs_3_, bf16[128,256]{1,0:T(8,128)(2,1)} %constant.19.clone.refs_4_, bf16[128,128]{1,0:T(8,128)(2,1)} %constant.20.clone.refs_5_, ...), custom_call_target="tpu_custom_call" | custom-call | tf_op jit(solution)/shard_map/fields/pallas_call | solution.py:613
  52.8 1.7 %copy.16 = f32[4,16384]{1,0:T(4,128)} copy(f32[4,16384]{1,0:T(4,128)} %bitcast.12) | data formatting | bytes 524288

commit v7 on v6

--- a/solution.py
+++ b/solution.py
@@ -166,6 +166,17 @@
         cols[2, o] = cell[0] + 2 * ox
         cols[3, o] = cell[1] + 2 * oy
     c["t_cols"] = cols.reshape(8, 1440)
+    far_x = coord[0][:, None] - cols[0].reshape(1440)[None, :]
+    far_y = coord[1][:, None] - cols[1].reshape(1440)[None, :]
+    gap = np.maximum(
+        np.abs(cell[0][:, None] - cols[2].reshape(1440)[None, :]),
+        np.abs(cell[1][:, None] - cols[3].reshape(1440)[None, :]),
+    )
+    inv = np.where(gap > 1.5, 1.0 / (far_x**2 + far_y**2 + SOFTEN), 0.0)
+    kx, ky = far_x * inv, far_y * inv
+    full = np.concatenate([kx, ky, ky * ky - kx * kx, -2.0 * kx * ky]).astype(np.float32)
+    c["hi_leaf"] = full.astype(BF16)
+    c["lo_leaf"] = (full - c["hi_leaf"].astype(np.float32)).astype(BF16)
     sides = np.zeros((8, HROWS), np.float32)
     for d, (dx, dy) in enumerate(DIRS):
         sides[0, ROW_OF[d] : ROW_OF[d] + ROWS_IN[d]] = dx
@@ -218,7 +229,7 @@
     out, refs = refs[0], refs[1:]
     held, refs = refs[:OPERANDS], refs[OPERANDS:]
     (pos, mass, count, src_leaf, sel_leaf, sel_mom, up, t_rows, t_cols, sides, src_mom,
-     down) = held
+     down, hi_leaf, lo_leaf) = held
     arrive_sems = refs[0]
     arrivals = [
         pltpu.make_async_copy(src, dst, arrive_sems.at[i])
@@ -227,13 +238,13 @@
     for i in (1, 2, 3, 0, *range(4, OPERANDS)):
         arrivals[i].start()
     run_kernel(dev_count, bits, arrivals, pos, mass, count, sel_leaf, sel_mom, up, down, sides,
-               src_leaf, src_mom, t_rows, t_cols, out, *refs[1:])
+               src_leaf, src_mom, t_rows, t_cols, hi_leaf, lo_leaf, out, *refs[1:])
 
 
 def run_kernel(dev_count, bits, arrivals, pos, mass, count, sel_leaf, sel_mom, up, down, sides,
-               src_leaf, src_mom, t_rows, t_cols, out, own, mom, send, recv, part, mid, leaf_mom, first,
-                 second, su, sv, sw, xs, xs_par, hi_leaf, lo_leaf, hi_par, lo_par, leaf_kind, leaf_local,
-                 result, edge_s, edge_r, sum_s1, sum_r1, sum_s2, sum_r2):
+               src_leaf, src_mom, t_rows, t_cols, hi_leaf, lo_leaf, out, own, mom, send, recv, part, mid, leaf_mom, first,
+                 second, su, sv, sw, lone, xs, xs_par, hi_par, lo_par, leaf_kind, leaf_local,
+                 result, self_live, edge_s, edge_r, sum_s1, sum_r1, sum_s2, sum_r2):
     code = lax.axis_index("grp") * dev_count + lax.axis_index("dev")
     bx, by = morton_split(code, bits)
     nx, ny = 2 ** ((bits + 1) // 2), 2 ** (bits // 2)
@@ -340,7 +351,7 @@
         own[k * PPL : (k + 1) * PPL, 0:128] = vals[:PPL]
         own[k * PPL : (k + 1) * PPL, 128:256] = vals[PPL:]
 
-    for arrival in arrivals[4:]:
+    for arrival in arrivals[4:12]:
         arrival.wait()
     leaf_mom[...] = jnp.zeros_like(leaf_mom)
     for tile in (0, 1):
@@ -424,7 +435,6 @@
         lax.fori_loop(0, 10, fill, 0)
 
     fill_tables(2.0, hi_par, lo_par)
-    fill_tables(1.0, hi_leaf, lo_leaf)
 
     def at_offset(o):
         return slice(o * PPL, o * PPL + PPL)
@@ -447,17 +457,12 @@
         lanes = slice(tile * 128, tile * 128 + 128)
         su[tile, self_at : self_at + PPL, :] = own[0:64, lanes] * 0.5
         sv[tile, self_at : self_at + PPL, :] = own[64:128, lanes] * 0.5
-        sw[tile, self_at : self_at + PPL, :] = own[128:192, lanes]
-
-    def targets(tile, base, width):
-        lanes = slice(tile * 128, tile * 128 + 128)
-        tx = [own[base + 8 * i : base + 8 * i + 8, lanes] * 0.5 for i in range(width)]
-        ty = [own[64 + base + 8 * i : 72 + base + 8 * i, lanes] * 0.5 for i in range(width)]
-        return tx, ty
+        m = own[128:192, lanes]
+        sw[tile, self_at : self_at + PPL, :] = jnp.where(m > 0.0, m - near_mean, 0.0)
+        lone[tile, 0:PPL, :] = jnp.where(m > 0.0, 1.0, 0.0)
 
     def near_field(first_row, row_count):
         width, unroll = 4, 16
-        zero = jnp.zeros((8, 128), F32)
         for tile in (0, 1):
             for piece in range(PPL // (8 * width)):
                 base = piece * 8 * width
@@ -491,6 +496,53 @@
                             near = near * -2.0
                         result[c, rows, :] = result[c, rows, :] + near
 
+    zero = jnp.zeros((8, 128), F32)
+
+    def targets(tile, base, width):
+        lanes = slice(tile * 128, tile * 128 + 128)
+        tx = [own[base + 8 * i : base + 8 * i + 8, lanes] * 0.5 for i in range(width)]
+        ty = [own[64 + base + 8 * i : 72 + base + 8 * i, lanes] * 0.5 for i in range(width)]
+        return tx, ty
+
+    self_width = 2
+    for tile in (0, 1):
+        for piece in range(PPL // (8 * self_width)):
+            base = piece * 8 * self_width
+            tx, ty = targets(tile, base, self_width)
+
+            def self_pairs(step, acc, tile=tile, tx=tx, ty=ty):
+                acc = list(acc)
+                for i in range(4):
+                    k = step * 4 + i
+                    at = pl.ds(self_at + k, 8, stride=0)
+                    sx, sy, m = su[tile, at, :], sv[tile, at, :], sw[tile, at, :]
+                    one = lone[tile, pl.ds(k, 8, stride=0), :]
+                    for t in range(self_width):
+                        dx = tx[t] - sx
+                        dy = ty[t] - sy
+                        x2 = dx * dx
+                        y2 = dy * dy
+                        inv = 1.0 / (x2 + y2 + SOFTEN)
+                        gap = y2 - x2
+                        cross = dx * dy
+                        for kind, w in enumerate((m, one)):
+                            at_acc = 8 * t + 4 * kind
+                            w1 = w * inv
+                            w2 = w1 * inv
+                            acc[at_acc] = acc[at_acc] + w1 * dx
+                            acc[at_acc + 1] = acc[at_acc + 1] + w1 * dy
+                            acc[at_acc + 2] = acc[at_acc + 2] + w2 * gap
+                            acc[at_acc + 3] = acc[at_acc + 3] + w2 * cross
+                return tuple(acc)
+
+            acc = lax.fori_loop(0, PPL // 4, self_pairs, (zero,) * (8 * self_width))
+            for t in range(self_width):
+                rows = slice(tile * PPL + base + 8 * t, tile * PPL + base + 8 * t + 8)
+                for c in range(4):
+                    scale = -2.0 if c == 3 else 1.0
+                    result[c, rows, :] = acc[8 * t + c] * scale
+                    self_live[c, rows, :] = acc[8 * t + 4 + c] * scale
+
     for copy in edges:
         copy.wait()
     cell_x = sides[0:1] + jnp.full((1, 128), bx, jnp.int32).astype(F32)
@@ -547,6 +599,8 @@
     from_par = jnp.dot(
         down[...], par_cols, precision=HIGHEST, preferred_element_type=F32
     )
+    for arrival in arrivals[12:]:
+        arrival.wait()
     wide = tn_none(hi_leaf[...], xs[...])
     leaf = wide[:, 0:128] + wide[:, 128:256] + tn_none(lo_leaf[...], xs[:, 0:128])
     for kind in (0, 1):
@@ -566,8 +620,8 @@
     live_sum = jnp.sum(sums[1:2], axis=1, keepdims=True)
     mean = mass_sum / live_sum
     for tile in (0, 1):
-        m = sw[tile, 0 : 9 * PPL, :]
-        sw[tile, 0 : 9 * PPL, :] = jnp.where(m > 0.0, m - mean, 0.0)
+        m = sw[tile, 0:self_at, :]
+        sw[tile, 0:self_at, :] = jnp.where(m > 0.0, m - mean, 0.0)
     for c in range(4):
         leaf_local[c] = leaf_kind[0, c] - (mean - near_mean) * leaf_kind[1, c]
 
@@ -577,15 +631,15 @@
         bv = basis(own[64:128, lanes])
         for c in range(4):
             rows = slice(tile * PPL, tile * PPL + PPL)
-            acc = None
+            acc = result[c, rows, :] - (mean - near_mean) * self_live[c, rows, :]
             for a in range(NODES):
                 half = leaf_local[c, pl.ds(a * 6, 1), lanes] * bv[0]
                 for b in range(1, NODES):
                     half = half + leaf_local[c, pl.ds(a * 6 + b, 1), lanes] * bv[b]
-                acc = half * bu[a] if acc is None else acc + half * bu[a]
+                acc = acc + half * bu[a]
             result[c, rows, :] = acc
 
-    near_field(0, 9 * PPL)
+    near_field(0, self_at)
 
     for c in range(4):
         back = result[c].T
@@ -597,7 +651,8 @@
     return pl.BlockSpec(memory_space=pltpu.VMEM)
 
 
-NAMES = ("src_leaf", "sel_leaf", "sel_mom", "up", "t_rows", "t_cols", "sides", "src_mom", "down")
+NAMES = ("src_leaf", "sel_leaf", "sel_mom", "up", "t_rows", "t_cols", "sides", "src_mom", "down",
+         "hi_leaf", "lo_leaf")
 OPERANDS = 3 + len(NAMES)
 
 
@@ -630,14 +685,14 @@
             pltpu.VMEM((2, 9 * PPL + 8, 128), F32),
             pltpu.VMEM((2, 9 * PPL + 8, 128), F32),
             pltpu.VMEM((2, 9 * PPL + 8, 128), F32),
+            pltpu.VMEM((2, PPL + 8, 128), F32),
             pltpu.VMEM((1440, 256), BF16),
             pltpu.VMEM((1440, 64), BF16),
             pltpu.VMEM((640, 1440), BF16),
             pltpu.VMEM((640, 1440), BF16),
-            pltpu.VMEM((640, 1440), BF16),
-            pltpu.VMEM((640, 1440), BF16),
             pltpu.VMEM((2, 4, NM, 256), F32),
             pltpu.VMEM((4, NM, 256), F32),
+            pltpu.VMEM((4, 128, 128), F32),
             pltpu.VMEM((4, 128, 128), F32),
             pltpu.SemaphoreType.DMA((8,)),
             pltpu.SemaphoreType.DMA((8,)),

time: 54.6 us -> 55.2 us (1.011)
  Pallas kernels: 52.8 us -> 53.4 us
    pallas_call x1, Pallas kernels: 52.8 us -> 53.4 us  [on_device(): pl.pallas_call(functools.partial(whole_kernel, dev_count, bits), out_shap...]
where the time goes in v7:
time: 55.2 us; the launch traced here: 55.1 us
  Pallas kernels  53.4 us (97%)
  local copies, waits for them, and re-layouts  1.67 us (3%)
    pallas_call x1, Pallas kernels, on_device(): pl.pallas_call(functools.partial(whole_kernel, dev_count, bits), out_shap...  53.4 us
    unnamed x1, local copies, waits for them, and re-layouts  1.67 us

profile of v7, /device:TPU:1, one launch (start us, length us, event | category | flops | bytes accessed | tf_op | source)
XLA Modules:
  0.0 55.1 jit_solution(3871234662343498615)
XLA Ops:
  0.0 53.4 %fields.1 = f32[512,128]{1,0:T(8,128)} custom-call(f32[256,128]{1,0:T(8,128)} %bitcast.13, f32[128,128]{1,0:T(8,128)} %bitcast.14, s32[2,128]{1,0:T(2,128)} %bitcast.15, s32[16,256]{1,0:T(8,128)} %constant.22.clone.refs_3_, bf16[128,256]{1,0:T(8,128)(2,1)} %constant.23.clone.refs_4_, bf16[128,128]{1,0:T(8,128)(2,1)} %constant.24.clone.refs_5_, ...), custom_call_target="tpu_custom_call" | custom-call | tf_op jit(solution)/shard_map/fields/pallas_call | solution.py:668
  53.4 1.7 %copy.18 = f32[4,16384]{1,0:T(4,128)} copy(f32[4,16384]{1,0:T(4,128)} %bitcast.12) | data formatting | bytes 524288

commit v8 on v7

--- a/solution.py
+++ b/solution.py
@@ -405,8 +405,6 @@
         copy.start()
         edges.append(copy)
     recv[96:HROWS, :] = jnp.zeros((HROWS - 96, LANES_OUT), F32)
-    mid[...] = lax.fori_loop(1, low_n, add_low, part[...])
-    lax.fori_loop(1, high_n, start_high, 0)
 
     def fill_tables(scale, table_hi, table_lo):
         def fill(i, carry):
@@ -495,6 +493,9 @@
                         if c == 3:
                             near = near * -2.0
                         result[c, rows, :] = result[c, rows, :] + near
+
+    mid[...] = lax.fori_loop(1, low_n, add_low, part[...])
+    lax.fori_loop(1, high_n, start_high, 0)
 
     zero = jnp.zeros((8, 128), F32)
 

time: 55.2 us -> 52.5 us (0.951)
  Pallas kernels: 53.4 us -> 50.7 us
    pallas_call x1, Pallas kernels: 53.4 us -> 50.7 us  [on_device(): pl.pallas_call(functools.partial(whole_kernel, dev_count, bits), out_shap...]
where the time goes in v8:
time: 52.5 us; the launch traced here: 52.4 us
  Pallas kernels  50.7 us (97%)
  local copies, waits for them, and re-layouts  1.67 us (3%)
    pallas_call x1, Pallas kernels, on_device(): pl.pallas_call(functools.partial(whole_kernel, dev_count, bits), out_shap...  50.7 us
    unnamed x1, local copies, waits for them, and re-layouts  1.67 us

profile of v8, /device:TPU:1, one launch (start us, length us, event | category | flops | bytes accessed | tf_op | source)
XLA Modules:
  0.0 52.4 jit_solution(5275774062298638611)
XLA Ops:
  0.0 50.7 %fields.1 = f32[512,128]{1,0:T(8,128)} custom-call(f32[256,128]{1,0:T(8,128)} %bitcast.13, f32[128,128]{1,0:T(8,128)} %bitcast.14, s32[2,128]{1,0:T(2,128)} %bitcast.15, s32[16,256]{1,0:T(8,128)} %constant.22.clone.refs_3_, bf16[128,256]{1,0:T(8,128)(2,1)} %constant.23.clone.refs_4_, bf16[128,128]{1,0:T(8,128)(2,1)} %constant.24.clone.refs_5_, ...), custom_call_target="tpu_custom_call" | custom-call | tf_op jit(solution)/shard_map/fields/pallas_call | solution.py:669
  50.7 1.7 %copy.18 = f32[4,16384]{1,0:T(4,128)} copy(f32[4,16384]{1,0:T(4,128)} %bitcast.12) | data formatting | bytes 524288

commit v9 on v8

--- a/solution.py
+++ b/solution.py
@@ -172,11 +172,13 @@
         np.abs(cell[0][:, None] - cols[2].reshape(1440)[None, :]),
         np.abs(cell[1][:, None] - cols[3].reshape(1440)[None, :]),
     )
-    inv = np.where(gap > 1.5, 1.0 / (far_x**2 + far_y**2 + SOFTEN), 0.0)
-    kx, ky = far_x * inv, far_y * inv
-    full = np.concatenate([kx, ky, ky * ky - kx * kx, -2.0 * kx * ky]).astype(np.float32)
-    c["hi_leaf"] = full.astype(BF16)
-    c["lo_leaf"] = (full - c["hi_leaf"].astype(np.float32)).astype(BF16)
+    for name, scale in (("leaf", 1.0), ("par", 2.0)):
+        sx, sy = far_x * scale, far_y * scale
+        inv = np.where(gap > 1.5, 1.0 / (sx**2 + sy**2 + SOFTEN), 0.0)
+        kx, ky = sx * inv, sy * inv
+        full = np.concatenate([kx, ky, ky * ky - kx * kx, -2.0 * kx * ky]).astype(np.float32)
+        c["hi_" + name] = full.astype(BF16)
+        c["lo_" + name] = (full - c["hi_" + name].astype(np.float32)).astype(BF16)
     sides = np.zeros((8, HROWS), np.float32)
     for d, (dx, dy) in enumerate(DIRS):
         sides[0, ROW_OF[d] : ROW_OF[d] + ROWS_IN[d]] = dx
@@ -229,7 +231,7 @@
     out, refs = refs[0], refs[1:]
     held, refs = refs[:OPERANDS], refs[OPERANDS:]
     (pos, mass, count, src_leaf, sel_leaf, sel_mom, up, t_rows, t_cols, sides, src_mom,
-     down, hi_leaf, lo_leaf) = held
+     down, hi_par, lo_par, hi_leaf, lo_leaf) = held
     arrive_sems = refs[0]
     arrivals = [
         pltpu.make_async_copy(src, dst, arrive_sems.at[i])
@@ -238,12 +240,12 @@
     for i in (1, 2, 3, 0, *range(4, OPERANDS)):
         arrivals[i].start()
     run_kernel(dev_count, bits, arrivals, pos, mass, count, sel_leaf, sel_mom, up, down, sides,
-               src_leaf, src_mom, t_rows, t_cols, hi_leaf, lo_leaf, out, *refs[1:])
+               src_leaf, src_mom, t_rows, t_cols, hi_par, lo_par, hi_leaf, lo_leaf, out, *refs[1:])
 
 
 def run_kernel(dev_count, bits, arrivals, pos, mass, count, sel_leaf, sel_mom, up, down, sides,
-               src_leaf, src_mom, t_rows, t_cols, hi_leaf, lo_leaf, out, own, mom, send, recv, part, mid, leaf_mom, first,
-                 second, su, sv, sw, lone, xs, xs_par, hi_par, lo_par, leaf_kind, leaf_local,
+               src_leaf, src_mom, t_rows, t_cols, hi_par, lo_par, hi_leaf, lo_leaf, out, own, mom, send, recv, part, mid, leaf_mom, first,
+                 second, su, sv, sw, lone, xs, xs_par, leaf_kind, leaf_local,
                  result, self_live, edge_s, edge_r, sum_s1, sum_r1, sum_s2, sum_r2):
     code = lax.axis_index("grp") * dev_count + lax.axis_index("dev")
     bx, by = morton_split(code, bits)
@@ -406,34 +408,6 @@
         edges.append(copy)
     recv[96:HROWS, :] = jnp.zeros((HROWS - 96, LANES_OUT), F32)
 
-    def fill_tables(scale, table_hi, table_lo):
-        def fill(i, carry):
-            at = pl.multiple_of(i * 16, 16)
-            rows = t_rows[pl.ds(at, 16), :]
-            row_x, row_y = rows[:, 0:1] * scale, rows[:, 1:2] * scale
-            cell_x, cell_y = rows[:, 2:3], rows[:, 3:4]
-            for start in range(0, 1440, FILL_LANES):
-                lanes = slice(start, min(start + FILL_LANES, 1440))
-                dx = row_x - t_cols[0:1, lanes] * scale
-                dy = row_y - t_cols[1:2, lanes] * scale
-                gap = jnp.maximum(
-                    jnp.abs(cell_x - t_cols[2:3, lanes]), jnp.abs(cell_y - t_cols[3:4, lanes])
-                )
-                x2 = dx * dx
-                y2 = dy * dy
-                inv = jnp.where(gap > 1.5, 1.0 / (x2 + y2 + SOFTEN), 0.0)
-                kx = dx * inv
-                ky = dy * inv
-                for c, val in enumerate((kx, ky, ky * ky - kx * kx, -2.0 * kx * ky)):
-                    hi, lo = split2(val)
-                    table_hi[pl.ds(c * 160 + at, 16), lanes] = hi
-                    table_lo[pl.ds(c * 160 + at, 16), lanes] = lo
-            return carry
-
-        lax.fori_loop(0, 10, fill, 0)
-
-    fill_tables(2.0, hi_par, lo_par)
-
     def at_offset(o):
         return slice(o * PPL, o * PPL + PPL)
 
@@ -586,6 +560,8 @@
     for o in range(9):
         shift_moments(o)
 
+    for arrival in arrivals[12:]:
+        arrival.wait()
     wide = tn_none(hi_par[...], xs_par[...])
     par = wide[:, 0:32] + wide[:, 32:64] + tn_none(lo_par[...], xs_par[:, 0:32])
     par_cols = jnp.concatenate(
@@ -600,8 +576,6 @@
     from_par = jnp.dot(
         down[...], par_cols, precision=HIGHEST, preferred_element_type=F32
     )
-    for arrival in arrivals[12:]:
-        arrival.wait()
     wide = tn_none(hi_leaf[...], xs[...])
     leaf = wide[:, 0:128] + wide[:, 128:256] + tn_none(lo_leaf[...], xs[:, 0:128])
     for kind in (0, 1):
@@ -653,7 +627,7 @@
 
 
 NAMES = ("src_leaf", "sel_leaf", "sel_mom", "up", "t_rows", "t_cols", "sides", "src_mom", "down",
-         "hi_leaf", "lo_leaf")
+         "hi_par", "lo_par", "hi_leaf", "lo_leaf")
 OPERANDS = 3 + len(NAMES)
 
 
@@ -689,8 +663,6 @@
             pltpu.VMEM((2, PPL + 8, 128), F32),
             pltpu.VMEM((1440, 256), BF16),
             pltpu.VMEM((1440, 64), BF16),
-            pltpu.VMEM((640, 1440), BF16),
-            pltpu.VMEM((640, 1440), BF16),
             pltpu.VMEM((2, 4, NM, 256), F32),
             pltpu.VMEM((4, NM, 256), F32),
             pltpu.VMEM((4, 128, 128), F32),

time: 52.5 us -> 52.5 us (level)
  no operation moved by 1% of the time
where the time goes in v9:
time: 52.5 us; the launch traced here: 52.4 us
  Pallas kernels  50.8 us (97%)
  local copies, waits for them, and re-layouts  1.67 us (3%)
    pallas_call x1, Pallas kernels, on_device(): pl.pallas_call(functools.partial(whole_kernel, dev_count, bits), out_shap...  50.8 us
    unnamed x1, local copies, waits for them, and re-layouts  1.67 us

profile of v9, /device:TPU:1, one launch (start us, length us, event | category | flops | bytes accessed | tf_op | source)
XLA Modules:
  0.0 52.4 jit_solution(7219481292113800286)
XLA Ops:
  0.0 50.8 %fields.1 = f32[512,128]{1,0:T(8,128)} custom-call(f32[256,128]{1,0:T(8,128)} %bitcast.13, f32[128,128]{1,0:T(8,128)} %bitcast.14, s32[2,128]{1,0:T(2,128)} %bitcast.15, s32[16,256]{1,0:T(8,128)} %constant.26.clone.refs_3_, bf16[128,256]{1,0:T(8,128)(2,1)} %constant.27.clone.refs_4_, bf16[128,128]{1,0:T(8,128)(2,1)} %constant.28.clone.refs_5_, ...), custom_call_target="tpu_custom_call" | custom-call | tf_op jit(solution)/shard_map/fields/pallas_call | solution.py:643
  50.8 1.7 %copy.20 = f32[4,16384]{1,0:T(4,128)} copy(f32[4,16384]{1,0:T(4,128)} %bitcast.12) | data formatting | bytes 524288

commit v10 on v9

--- a/solution.py
+++ b/solution.py
@@ -468,9 +468,6 @@
                             near = near * -2.0
                         result[c, rows, :] = result[c, rows, :] + near
 
-    mid[...] = lax.fori_loop(1, low_n, add_low, part[...])
-    lax.fori_loop(1, high_n, start_high, 0)
-
     zero = jnp.zeros((8, 128), F32)
 
     def targets(tile, base, width):
@@ -481,6 +478,9 @@
 
     self_width = 2
     for tile in (0, 1):
+        if tile == 1:
+            mid[...] = lax.fori_loop(1, low_n, add_low, part[...])
+            lax.fori_loop(1, high_n, start_high, 0)
         for piece in range(PPL // (8 * self_width)):
             base = piece * 8 * self_width
             tx, ty = targets(tile, base, self_width)

time: 52.5 us -> 51.7 us (0.985)
  Pallas kernels: 50.8 us -> 49.9 us
    pallas_call x1, Pallas kernels: 50.8 us -> 49.9 us  [on_device(): pl.pallas_call(functools.partial(whole_kernel, dev_count, bits), out_shap...]
where the time goes in v10:
time: 51.7 us; the launch traced here: 51.6 us
  Pallas kernels  49.9 us (97%)
  local copies, waits for them, and re-layouts  1.67 us (3%)
    pallas_call x1, Pallas kernels, on_device(): pl.pallas_call(functools.partial(whole_kernel, dev_count, bits), out_shap...  49.9 us
    unnamed x1, local copies, waits for them, and re-layouts  1.67 us

profile of v10, /device:TPU:1, one launch (start us, length us, event | category | flops | bytes accessed | tf_op | source)
XLA Modules:
  0.0 51.6 jit_solution(14959694288610365347)
XLA Ops:
  0.0 49.9 %fields.1 = f32[512,128]{1,0:T(8,128)} custom-call(f32[256,128]{1,0:T(8,128)} %bitcast.13, f32[128,128]{1,0:T(8,128)} %bitcast.14, s32[2,128]{1,0:T(2,128)} %bitcast.15, s32[16,256]{1,0:T(8,128)} %constant.26.clone.refs_3_, bf16[128,256]{1,0:T(8,128)(2,1)} %constant.27.clone.refs_4_, bf16[128,128]{1,0:T(8,128)(2,1)} %constant.28.clone.refs_5_, ...), custom_call_target="tpu_custom_call" | custom-call | tf_op jit(solution)/shard_map/fields/pallas_call | solution.py:643
  49.9 1.7 %copy.20 = f32[4,16384]{1,0:T(4,128)} copy(f32[4,16384]{1,0:T(4,128)} %bitcast.12) | data formatting | bytes 524288

commit v11 on v10

--- a/solution.py
+++ b/solution.py
@@ -20,6 +20,7 @@
 DIRS = ((-1, 0), (1, 0), (0, -1), (0, 1), (-1, -1), (1, -1), (-1, 1), (1, 1))
 ROW_OF = (0, 16, 32, 48, 64, 72, 80, 88)
 ROWS_IN = (16, 16, 16, 16, 8, 8, 8, 8)
+ROWS_SENT = (16, 16, 16, 16, 2, 2, 2, 2)
 HROWS = 128
 LANES_OUT = 512
 OFFS = tuple((ox, oy) for ox in (-1, 0, 1) for oy in (-1, 0, 1) if (ox, oy) != (0, 0)) + ((0, 0),)
@@ -279,6 +280,7 @@
         greet(in_high(k))
         return carry
 
+    recv[64:HROWS, :] = jnp.zeros((HROWS - 64, LANES_OUT), F32)
     lax.fori_loop(1, low_n, greet_low, 0)
     for dx, dy in DIRS:
         greet(beside(dx, dy))
@@ -398,7 +400,7 @@
     )
     edges = []
     for d, (dx, dy) in enumerate(DIRS):
-        rows = pl.ds(ROW_OF[d], ROWS_IN[d])
+        rows = pl.ds(ROW_OF[d], ROWS_SENT[d])
         copy = pltpu.make_async_remote_copy(
             src_ref=send.at[rows], dst_ref=recv.at[rows], send_sem=edge_s.at[d],
             recv_sem=edge_r.at[d], device_id=beside(-dx, -dy),
@@ -406,7 +408,6 @@
         )
         copy.start()
         edges.append(copy)
-    recv[96:HROWS, :] = jnp.zeros((HROWS - 96, LANES_OUT), F32)
 
     def at_offset(o):
         return slice(o * PPL, o * PPL + PPL)

time: 51.7 us -> 51.2 us (level)
    pallas_call x1, Pallas kernels: 49.9 us -> 49.4 us  [on_device(): pl.pallas_call(functools.partial(whole_kernel, dev_count, bits), out_shap...]
where the time goes in v11:
time: 51.2 us; the launch traced here: 51.1 us
  Pallas kernels  49.4 us (96%)
  local copies, waits for them, and re-layouts  1.67 us (3%)
    pallas_call x1, Pallas kernels, on_device(): pl.pallas_call(functools.partial(whole_kernel, dev_count, bits), out_shap...  49.4 us
    unnamed x1, local copies, waits for them, and re-layouts  1.67 us

profile of v11, /device:TPU:1, one launch (start us, length us, event | category | flops | bytes accessed | tf_op | source)
XLA Modules:
  0.0 51.1 jit_solution(7882622562446466028)
XLA Ops:
  0.0 49.4 %fields.1 = f32[512,128]{1,0:T(8,128)} custom-call(f32[256,128]{1,0:T(8,128)} %bitcast.13, f32[128,128]{1,0:T(8,128)} %bitcast.14, s32[2,128]{1,0:T(2,128)} %bitcast.15, s32[16,256]{1,0:T(8,128)} %constant.26.clone.refs_3_, bf16[128,256]{1,0:T(8,128)(2,1)} %constant.27.clone.refs_4_, bf16[128,128]{1,0:T(8,128)(2,1)} %constant.28.clone.refs_5_, ...), custom_call_target="tpu_custom_call" | custom-call | tf_op jit(solution)/shard_map/fields/pallas_call | solution.py:644
  49.4 1.7 %copy.20 = f32[4,16384]{1,0:T(4,128)} copy(f32[4,16384]{1,0:T(4,128)} %bitcast.12) | data formatting | bytes 524288

commit v12 on v11

--- a/solution.py
+++ b/solution.py
@@ -281,10 +281,10 @@
         return carry
 
     recv[64:HROWS, :] = jnp.zeros((HROWS - 64, LANES_OUT), F32)
-    lax.fori_loop(1, low_n, greet_low, 0)
+    lax.fori_loop(1, low_n, greet_low, 0, unroll=True)
     for dx, dy in DIRS:
         greet(beside(dx, dy))
-    lax.fori_loop(1, high_n, greet_high, 0)
+    lax.fori_loop(1, high_n, greet_high, 0, unroll=True)
 
     starts = [qx * 2 + qy * 4 + sy for sy in (0, 1) for qx in (0, 1) for qy in (0, 1)]
 
@@ -348,7 +348,7 @@
         return acc + second[k]
 
     pl.semaphore_wait(barrier, 8 + low_n - 1 + high_n - 1)
-    lax.fori_loop(1, low_n, start_low, 0)
+    lax.fori_loop(1, low_n, start_low, 0, unroll=True)
     arrivals[0].wait()
     for k in (0, 1):
         vals = turned(pos, k, 2)
@@ -480,8 +480,8 @@
     self_width = 2
     for tile in (0, 1):
         if tile == 1:
-            mid[...] = lax.fori_loop(1, low_n, add_low, part[...])
-            lax.fori_loop(1, high_n, start_high, 0)
+            mid[...] = lax.fori_loop(1, low_n, add_low, part[...], unroll=True)
+            lax.fori_loop(1, high_n, start_high, 0, unroll=True)
         for piece in range(PPL // (8 * self_width)):
             base = piece * 8 * self_width
             tx, ty = targets(tile, base, self_width)
@@ -591,7 +591,7 @@
                 axis=1,
             )
 
-    sums = lax.fori_loop(1, high_n, add_high, mid[...])
+    sums = lax.fori_loop(1, high_n, add_high, mid[...], unroll=True)
     mass_sum = jnp.sum(sums[0:1], axis=1, keepdims=True)
     live_sum = jnp.sum(sums[1:2], axis=1, keepdims=True)
     mean = mass_sum / live_sum

time: 51.2 us -> 51 us (level)
  no operation moved by 1% of the time
where the time goes in v12:
time: 51 us; the launch traced here: 50.9 us
  Pallas kernels  49.2 us (96%)
  local copies, waits for them, and re-layouts  1.67 us (3%)
    pallas_call x1, Pallas kernels, on_device(): pl.pallas_call(functools.partial(whole_kernel, dev_count, bits), out_shap...  49.2 us
    unnamed x1, local copies, waits for them, and re-layouts  1.67 us

profile of v12, /device:TPU:1, one launch (start us, length us, event | category | flops | bytes accessed | tf_op | source)
XLA Modules:
  0.0 50.9 jit_solution(10723747145251611931)
XLA Ops:
  0.0 49.2 %fields.1 = f32[512,128]{1,0:T(8,128)} custom-call(f32[256,128]{1,0:T(8,128)} %bitcast.13, f32[128,128]{1,0:T(8,128)} %bitcast.14, s32[2,128]{1,0:T(2,128)} %bitcast.15, s32[16,256]{1,0:T(8,128)} %constant.26.clone.refs_3_, bf16[128,256]{1,0:T(8,128)(2,1)} %constant.27.clone.refs_4_, bf16[128,128]{1,0:T(8,128)(2,1)} %constant.28.clone.refs_5_, ...), custom_call_target="tpu_custom_call" | custom-call | tf_op jit(solution)/shard_map/fields/pallas_call | solution.py:644
  49.2 1.7 %copy.20 = f32[4,16384]{1,0:T(4,128)} copy(f32[4,16384]{1,0:T(4,128)} %bitcast.12) | data formatting | bytes 524288
